TPU v7x, 32 devices: a whole 2x2x4 slice. The times are simulated.
32 devices in a mesh: stream: 2 (over y), dp: 16 (over z, x, core).
Axes of the slice: x: 2, y: 2, z: 4, core: 2. Of those that a mesh axis runs over, the one named last changes fastest.
Arguments:
- tokens: bfloat16 [2, 16384, 768], P('stream', 'dp'), may hold values from -40 to 40, as said below
- first_gain: float32 [2, 768], P('stream'), may hold values from 0.25 to 1.75
- first_shift: float32 [2, 768], P('stream'), may hold values from -1.5 to 1.5
- query_weight: bfloat16 [2, 768, 768], P('stream'), may hold values from -0.21875 to 0.21875
- query_bias: float32 [2, 768], P('stream'), may hold values from -1.5 to 1.5
- key_weight: bfloat16 [2, 768, 768], P('stream'), may hold values from -0.21875 to 0.21875
- value_weight: bfloat16 [2, 768, 768], P('stream'), may hold values from -0.21875 to 0.21875
- value_bias: float32 [2, 768], P('stream'), may hold values from -0.5 to 0.5
- out_weight: bfloat16 [2, 768, 768], P('stream'), may hold values from -1.75 to 1.75
- out_bias: float32 [2, 768], P('stream'), may hold values from -1.5 to 1.5
- second_gain: float32 [2, 768], P('stream'), may hold values from 0.25 to 1.75
- second_shift: float32 [2, 768], P('stream'), may hold values from -1.5 to 1.5
- up_weight: bfloat16 [2, 768, 3072], P('stream'), may hold values from -0.21875 to 0.21875
- up_bias: float32 [2, 3072], P('stream'), may hold values from -1.5 to 1.5
- down_weight: bfloat16 [2, 3072, 768], P('stream'), may hold values from -0.109375 to 0.109375
- down_bias: float32 [2, 768], P('stream'), may hold values from -1.5 to 1.5
- box_table: float32 [2, 768], P('stream'), may hold values from -4 to 4
- segments: int32 [2, 32, 512], P(None, 'dp'), may hold values from 0 to 63, never falling along the last dimension, each value on 1 to 16 neighbouring positions
- validity: int32 [2, 32, 512], P(None, 'dp'), may hold values from 0 to 1, as said below
- seg_boxes: int32 [32, 64, 4], P('dp'), may hold values from 0 to 1023
- cotangent: bfloat16 [2, 16384, 768], P('stream', 'dp'), may hold values from -6 to 6
Outputs:
- layer_out: bfloat16 [2, 16384, 768], P('stream', 'dp')
- grad_tokens: float32 [2, 16384, 768], P('stream', 'dp')
- grad_first_gain: float32 [2, 768], P('stream', 'dp')
- grad_first_shift: float32 [2, 768], P('stream', 'dp')
- grad_query_weight: float32 [2, 768, 768], P('stream', 'dp')
- grad_query_bias: float32 [2, 768], P('stream', 'dp')
- grad_key_weight: float32 [2, 768, 768], P('stream', 'dp')
- grad_value_weight: float32 [2, 768, 768], P('stream', 'dp')
- grad_value_bias: float32 [2, 768], P('stream', 'dp')
- grad_out_weight: float32 [2, 768, 768], P('stream', 'dp')
- grad_out_bias: float32 [2, 768], P('stream', 'dp')
- grad_second_gain: float32 [2, 768], P('stream', 'dp')
- grad_second_shift: float32 [2, 768], P('stream', 'dp')
- grad_up_weight: float32 [2, 768, 3072], P('stream', 'dp')
- gradient_expand_bias: float32 [2, 3072], P('stream', 'dp')
- grad_down_weight: float32 [2, 3072, 768], P('stream', 'dp')
- grad_down_bias: float32 [2, 768], P('stream', 'dp')
- grad_box_table: float32 [2, 768], P('stream', 'dp')
- root_means: float32 [2, 3], P('stream')
Inputs may be any that keep to these rules, and one draw needn't show every extreme that they name: `tokens`: activations of both streams. `validity`: in each page of each stream the valid tokens come first, 256 of them or more. `segments`: within a page of a stream the segment numbers never fall; a segment spans 1 to 16 tokens.
All inputs are finite; a program needn't handle non-finite values.
Results may differ from a plain program's by a relative error of at most 0.012.
The roundings to bfloat16 on the way count: a program that leaves them out, or rounds other values in their place, can miss the bound.
Values may be sent and summed in bfloat16 or wider, within the bound.
No kernel may reach another device: no remote copies, remote signals or barrier semaphores. Data moves between devices by JAX's collectives and lax.ppermute only.
A program may use at most 192 MiB of HBM per device.

v0:
```python
import functools

import jax
import jax.numpy as jnp
from jax import lax
from jax.experimental import pallas as pl
from jax.experimental.pallas import tpu as pltpu
from jax.sharding import PartitionSpec as P

HEADS = 12
BUCKETS = 32
SMALL = 24

score_scale = 0.125
norm_eps = 1e-05
mask_fill = -1000000000.0
box_step = 32
precise_variant = lax.Precision.HIGHEST
f32 = jnp.float32
bf16 = jnp.bfloat16


def nn(a, b):
    return lax.dot_general(a, b, (((1,), (0,)), ((), ())), preferred_element_type=f32)


def nt(a, b):
    return lax.dot_general(a, b, (((1,), (1,)), ((), ())), preferred_element_type=f32)


def tn(a, b):
    return lax.dot_general(a, b, (((0,), (0,)), ((), ())), preferred_element_type=f32)


def normal_rows(rows):
    centre = rows - jnp.mean(rows, -1, keepdims=True)
    spread = jnp.mean(centre * centre, -1, keepdims=True)
    scale = lax.rsqrt(spread + norm_eps)
    return centre * scale, scale


def params(mib=60):
    return pltpu.CompilerParams(vmem_limit_bytes=mib * 1024 * 1024)


def cost(flops, moved, trans=0, scale=1 / 64):
    return pl.CostEstimate(
        flops=int(flops * scale),
        bytes_accessed=int(moved * scale),
        transcendentals=int(trans * scale),
    )


def full(shape):
    zeros = (0,) * len(shape)
    return pl.BlockSpec(shape, lambda *_: zeros)


def query_kernel(x_ref, gain_ref, shift_ref, w_ref, b_ref, n_ref, q_ref):
    norm, _ = normal_rows(x_ref[...].astype(f32))
    low = (norm * gain_ref[...] + shift_ref[...]).astype(bf16)
    n_ref[...] = low
    query = (nn(low, w_ref[...]) + b_ref[...]).astype(bf16)
    q_ref[...] = (query.astype(f32) * score_scale).astype(bf16)


def query_call(x, gain, shift, weight, bias):
    length, width = x.shape
    tile = 256
    rows = pl.BlockSpec((tile, width), lambda i: (i, 0))
    return pl.pallas_call(
        query_kernel,
        grid=(length // tile,),
        in_specs=[rows, full((1, width)), full((1, width)), full(weight.shape), full((1, width))],
        out_specs=[rows, rows],
        out_shape=[jax.ShapeDtypeStruct(x.shape, bf16)] * 2,
        compiler_params=params(),
        cost_estimate=cost(2 * length * width * width, 6 * length * width + 2 * width * width),
        name="query",
    )(x, gain, shift, weight, bias)


def pair_kernel(me_ref, x_ref, rows_ref, *rest, count):
    pieces, (n_ref, k_ref, v_ref, copy_ref, w_ref) = rest[:count], rest[-5:]
    if count == 4:

        @pl.when(pl.program_id(0) == 0)
        def _():
            low = me_ref[0] & 3
            for place in range(4):
                w_ref[place ^ low] = pieces[place][...]

        weights = w_ref
    else:
        weights = pieces[0]
    half = weights.shape[1]
    copy_ref[...] = x_ref[...]
    norm, _ = normal_rows(x_ref[...].astype(f32))
    low = (norm * rows_ref[0:1, :] + rows_ref[1:2, :]).astype(bf16)
    n_ref[...] = low
    left, right = low[:, :half], low[:, half:]
    k_ref[...] = (nn(left, weights[0]) + nn(right, weights[1])).astype(bf16)
    v_ref[...] = (nn(left, weights[2]) + nn(right, weights[3]) + rows_ref[2:3, :]).astype(bf16)


def pair_call(page, length, me, x, rows, pieces, before):
    page_len, width = x.shape
    tile = 256
    first = page * page_len // tile
    placed = pl.BlockSpec((tile, width), lambda i, *_: (i + first, 0))
    left = pl.BlockSpec(memory_space=pl.ANY)
    weights = (4, width // 2, width)
    out_specs = [placed] * 4
    shapes = [jax.ShapeDtypeStruct((length, width), bf16)] * 4
    scratch = []
    if len(pieces) == 4:
        out_specs = out_specs + [full(weights)]
        shapes = shapes + [jax.ShapeDtypeStruct(weights, bf16)]
    else:
        scratch = [pltpu.VMEM((8, 128), f32)]
    grid_spec = pltpu.PrefetchScalarGridSpec(
        num_scalar_prefetch=1,
        grid=(page_len // tile,),
        in_specs=[
            pl.BlockSpec((tile, width), lambda i, *_: (i, 0)),
            full(rows.shape),
        ]
        + [full(piece.shape) for piece in pieces]
        + [left] * len(before),
        out_specs=out_specs,
        scratch_shapes=scratch,
    )
    return pl.pallas_call(
        functools.partial(pair_kernel, count=len(pieces)),
        grid_spec=grid_spec,
        out_shape=shapes,
        input_output_aliases={3 + len(pieces) + i: i for i in range(len(before))},
        compiler_params=params(),
        cost_estimate=cost(4 * page_len * width * width, 8 * page_len * width),
        name="pair",
    )(me, x, rows, *pieces, *before)


def head_lanes(value, head, head_dim):
    lane = lax.broadcasted_iota(jnp.int32, value.shape, 1)
    mine = (lane >= head * head_dim) & (lane < (head + 1) * head_dim)
    return jnp.where(mine, value, jnp.zeros_like(value))


def picks_kernel(hq_ref, bias_ref, out_ref):
    for pair in range(out_ref.shape[1] // 256):
        both = jnp.concatenate([bias_ref[0, 2 * pair], bias_ref[0, 2 * pair + 1]], 1)
        out_ref[:, 256 * pair : 256 * (pair + 1)] = nn(hq_ref[0], both).astype(bf16)


def picks_call(hot_q, bias):
    pages, page_len = hot_q.shape[0], hot_q.shape[1]
    return pl.pallas_call(
        picks_kernel,
        grid=(pages, 3),
        in_specs=[
            pl.BlockSpec((1, page_len, 64), lambda p, h: (p, 0, 0)),
            pl.BlockSpec((1, 4, 64, 128), lambda p, h: (p, h, 0, 0)),
        ],
        out_specs=pl.BlockSpec((page_len, 512), lambda p, h: (p, h)),
        out_shape=jax.ShapeDtypeStruct((pages * page_len, HEADS * 128), bf16),
        compiler_params=params(),
        cost_estimate=cost(2 * pages * page_len * HEADS * 128 * 64, pages * page_len * HEADS * 256),
        name="picks",
    )(hot_q, bias)


def pair_right(q, picks):
    heads = [head_lanes(q, head, 64) for head in range(2)]
    sides = [
        jnp.concatenate([heads[head], picks[:, 128 * head : 128 * (head + 1)]], 1)
        for head in range(2)
    ]
    return jnp.concatenate(heads, 0), jnp.concatenate(sides, 0)


def attend_kernel(q_ref, k_ref, v_ref, picks_ref, hk_ref, *rest):
    o_ref, lse_ref = rest[-2:]
    page_len = q_ref.shape[0]
    for pair in range(q_ref.shape[1] // 128):
        lanes = slice(128 * pair, 128 * (pair + 1))
        left = jnp.concatenate([k_ref[:, lanes], hk_ref[0]], 1)
        v_turned = v_ref[:, lanes].astype(f32).T.astype(bf16)
        _, right = pair_right(q_ref[:, lanes], picks_ref[:, 256 * pair : 256 * (pair + 1)])
        scores = nt(left, right)
        peak = jnp.max(scores, 0, keepdims=True)
        raised = jnp.exp(scores - peak)
        total = jnp.sum(raised, 0, keepdims=True)
        probs = (raised * (1.0 / total)).astype(bf16)
        lse = peak + jnp.log(total)
        parts = []
        for head in range(2):
            mine = slice(head * page_len, (head + 1) * page_len)
            parts.append(nn(v_turned[head * 64 : (head + 1) * 64], probs[:, mine]))
            lse_ref[0, pair, head : head + 1, :] = lse[:, mine]
        o_ref[:, lanes] = jnp.concatenate(parts, 0).T.astype(bf16)


PAIRS = 2


def attend_specs(page_len, page, first):
    rows = pl.BlockSpec((page_len, 128 * PAIRS), lambda p, h: (p + page, h + first))
    picks = pl.BlockSpec((page_len, 256 * PAIRS), lambda p, h: (p + page, h + first))
    lse = pl.BlockSpec((1, PAIRS, 2, page_len), lambda p, h: (p + page, h + first, 0, 0))

    def hot(*shape):
        return pl.BlockSpec((1,) + shape, lambda p, h: (p + page, 0, 0))

    return rows, picks, lse, hot


def attend_call(page, q, k, v, picks, hot_k, before):
    length, width = q.shape
    pages, page_len = hot_k.shape[0], hot_k.shape[1]
    rows, picks_spec, lse, hot = attend_specs(page_len, page, 0)
    left = pl.BlockSpec(memory_space=pl.ANY)
    return pl.pallas_call(
        attend_kernel,
        grid=(1, width // 128 // PAIRS),
        in_specs=[rows, rows, rows, picks_spec, hot(page_len, 128)] + [left] * len(before),
        out_specs=[rows, lse],
        out_shape=[
            jax.ShapeDtypeStruct((length, width), bf16),
            jax.ShapeDtypeStruct((pages, width // 128, 2, page_len), f32),
        ],
        input_output_aliases={5 + i: i for i in range(len(before))},
        compiler_params=params(),
        cost_estimate=cost(
            16 * page_len * page_len * width,
            8 * page_len * width,
            page_len * page_len * HEADS,
        ),
        name="attend",
    )(q, k, v, picks, hot_k, *before)


def attend_back_kernel(
    q_ref,
    k_ref,
    v_ref,
    picks_ref,
    hq_ref,
    hk_ref,
    hkt_ref,
    lse_ref,
    o_ref,
    do_ref,
    dq_ref,
    dk_ref,
    dv_ref,
    gb_ref,
):
    page_len = q_ref.shape[0]
    row = lax.broadcasted_iota(jnp.int32, (8, 128), 0)
    lane = lax.broadcasted_iota(jnp.int32, (8, 128), 1)
    chooser = (row == lane // 64).astype(bf16)
    for pair in range(q_ref.shape[1] // 128):
        lanes = slice(128 * pair, 128 * (pair + 1))
        k, v, do = k_ref[:, lanes], v_ref[:, lanes], do_ref[:, lanes]
        left = jnp.concatenate([k, hk_ref[0]], 1)
        k_turned = k.astype(f32).T.astype(bf16)
        overlap = do.astype(f32) * o_ref[:, lanes].astype(f32)
        high = overlap.astype(bf16)
        rest = (overlap - high.astype(f32)).astype(bf16)
        delta = nt(chooser, high) + nt(chooser, rest)
        delta = jnp.concatenate([delta[0:1], delta[1:2]], 1)
        lse = jnp.concatenate([lse_ref[0, pair, 0:1, :], lse_ref[0, pair, 1:2, :]], 1)
        queries, right = pair_right(q_ref[:, lanes], picks_ref[:, 256 * pair : 256 * (pair + 1)])
        do_heads = jnp.concatenate([head_lanes(do, head, 64) for head in range(2)], 0)
        probs = jnp.exp(nt(left, right) - lse)
        turn = (probs * (nt(v, do_heads) - delta)).astype(bf16)
        dv_ref[:, lanes] = nn(probs.astype(bf16), do_heads).astype(bf16)
        dk_ref[:, lanes] = nn(turn, queries).astype(bf16)
        parts, sums = [], []
        for head in range(2):
            both = nn(
                jnp.concatenate([k_turned[head * 64 : (head + 1) * 64], hkt_ref[0]], 0),
                turn[:, head * page_len : (head + 1) * page_len],
            )
            parts.append(both[:64])
            sums.append(both[64:])
        dq_ref[:, lanes] = (jnp.concatenate(parts, 0) * score_scale).T.astype(bf16)
        sums = jnp.concatenate(sums, 0)
        high = sums.astype(bf16)
        rest = (sums - high.astype(f32)).astype(bf16)
        grads = nn(jnp.concatenate([high, rest], 0), hq_ref[0])
        grads = grads[:128] + grads[128:]
        for head in range(2):
            gb_ref[0, 2 * pair + head] = grads[64 * head : 64 * (head + 1)]


def attend_back_call(pair, pairs, q, k, v, picks, hot_q, hot_k, hot_kt, lse_in, o, do):
    length, width = q.shape
    pages, page_len = hot_q.shape[0], hot_q.shape[1]
    rows, picks_spec, lse, hot = attend_specs(page_len, 0, pair // PAIRS)
    given = pl.BlockSpec((page_len, 128 * PAIRS), lambda p, h: (p, h))
    grad_bias = pl.BlockSpec((1, 2 * PAIRS, 64, 64), lambda p, h: (p, h, 0, 0))
    wide = jax.ShapeDtypeStruct((length, pairs * 128), bf16)
    return pl.pallas_call(
        attend_back_kernel,
        grid=(pages, pairs // PAIRS),
        in_specs=[
            rows,
            rows,
            rows,
            picks_spec,
            hot(page_len, 64),
            hot(page_len, 128),
            hot(64, page_len),
            lse,
            rows,
            rows,
        ],
        out_specs=[given, given, given, grad_bias],
        out_shape=[wide, wide, wide, jax.ShapeDtypeStruct((pages, 2 * pairs, 64, 64), f32)],
        compiler_params=params(),
        cost_estimate=cost(
            40 * length * page_len * pairs * 128,
            16 * length * pairs * 128,
            length * page_len * 2 * pairs,
            64,
        ),
        name="attend_back",
    )(q, k, v, picks, hot_q, hot_k, hot_kt, lse_in, o, do)


def put_rows(
    scratch, keep, send, me, relative, at, x_step, z_step, lanes=slice(None), source=slice(None)
):
    if not relative:
        keep[pl.ds(at, scratch.shape[0]), lanes] = scratch[:, source].astype(bf16)
        return
    step = scratch.shape[0] // 16
    for place in range(16):
        owner = place ^ me
        rows = scratch[pl.ds(pl.multiple_of(owner * step, step), step), source].astype(bf16)
        target = send if place & 1 else keep
        z = ((place >> 2) & 1) * 2 + (place >> 3)
        low = at + ((place >> 1) & 1) * x_step + z * z_step
        target[pl.ds(pl.multiple_of(low, 16), step), lanes] = rows


def put_quarter(scratch, keep, send, me, relative, at, x_step):
    if not relative:
        keep[pl.ds(at, scratch.shape[0]), :] = scratch[...].astype(bf16)
        return
    step = scratch.shape[0] // 4
    for place in range(4):
        owner = place ^ (me & 3)
        rows = scratch[pl.ds(pl.multiple_of(owner * step, step), step), :].astype(bf16)
        target = send if place & 1 else keep
        target[pl.ds(pl.multiple_of(at + (place >> 1) * x_step, 16), step), :] = rows


def block_shapes(rows, width, relative):
    if relative:
        return (rows // 2, width), (rows // 2, width)
    return (rows, width), (16, 128)


def feed_kernel(me_ref, *rest, first, blocks, relative, tile):
    ins, rest = rest[: 12 if first else 6], rest[12 if first else 8 :]
    if first:
        x_ref, mixed_ref, keep_ref, wo_ref, bo_ref, gain_ref, shift_ref = ins[:7]
        cot_ref, up_ref, upb_ref, down_ref, old_ref = ins[7:]
        middle_ref, n2_ref = rest[:2]
        rest = rest[2:]
    else:
        n2_ref, cot_ref, up_ref, upb_ref, down_ref, old_ref = ins
    act_ref, gh_ref, small_ref, kept_ref, sent_ref, dw_ref = rest[-6:]
    step = pl.program_id(0)
    length = cot_ref.shape[0]

    @pl.when(step == 0)
    def _():
        small_ref[...] = old_ref[...]
        if first:

            @pl.loop(0, length // 256)
            def _(i):
                at = pl.ds(pl.multiple_of(i * 256, 256), 256)
                branch = nn(mixed_ref[at, :], wo_ref[...]) + bo_ref[...]
                middle = x_ref[at, :].astype(f32) + branch
                middle_ref[at, :] = middle
                norm, _ = normal_rows(middle)
                n2_ref[at, :] = (norm * gain_ref[...] + shift_ref[...]).astype(bf16)
                small_ref[21:22, :] += jnp.sum(branch * branch * keep_ref[at, :], 0, keepdims=True)
                small_ref[23:24, :] += jnp.broadcast_to(
                    jnp.sum(keep_ref[at, :], 0, keepdims=True), (1, small_ref.shape[1])
                )

    row = (0 if first else blocks) + 16 + step

    @pl.loop(0, length // tile)
    def _(i):
        at = pl.ds(pl.multiple_of(i * tile, tile), tile)
        hidden = nn(n2_ref[at, :], up_ref[...]) + upb_ref[...]
        slope = nt(cot_ref[at, :], down_ref[...])
        gate = 0.5 * (1.0 + lax.erf(hidden * 0.7071067811865476))
        bell = jnp.exp(hidden * hidden * -0.5) * 0.3989422804014327
        act_ref[at, :] = (hidden * gate).astype(bf16)
        gh = (slope * (gate + hidden * bell)).astype(bf16)
        gh_ref[at, :] = gh
        small_ref[pl.ds(row, 1), :] += jnp.sum(gh.astype(f32), 0, keepdims=True)

    me = me_ref[0]
    width = dw_ref.shape[0]
    up_at, down_at = (step * 48, step * 192) if relative else (step * 2 * width, 0)
    dw_ref[...] = tn(n2_ref[...], gh_ref[...])
    up_steps = (96, 192) if first else (768, 96)
    put_rows(dw_ref, kept_ref, sent_ref, me, relative, up_at, *up_steps)
    dw_ref[...] = tn(act_ref[...], cot_ref[...])
    if relative:
        down_at = down_at + (768 if first else 384)
    else:
        down_at = up_at + width
    put_quarter(dw_ref, kept_ref, sent_ref, me, relative, down_at, 384 if first else 768)


def feed_call(part, parts, me, given, cot, up, upb, down, small, before, relative):
    length, width = cot.shape
    first = part == 0
    hidden = up.shape[1]
    blocks = hidden // width // parts
    start = part * blocks
    whole, row = full((length, width)), full((1, width))
    kept, sent = block_shapes(2 * width * blocks, width, relative)
    shape = jax.ShapeDtypeStruct
    if first:
        specs = [whole, whole, full((length, 1)), full((width, width)), row, row, row]
        outs = [whole, whole]
        shapes = [shape((length, width), f32), shape((length, width), bf16)]
    else:
        specs, outs, shapes = [whole], [], []
    columns = pl.BlockSpec((length, width), lambda j, *_: (0, j + start))
    left = pl.BlockSpec(memory_space=pl.ANY)
    grid_spec = pltpu.PrefetchScalarGridSpec(
        num_scalar_prefetch=1,
        grid=(blocks,),
        in_specs=specs
        + [
            whole,
            pl.BlockSpec((width, width), lambda j, *_: (0, j + start)),
            pl.BlockSpec((1, width), lambda j, *_: (0, j + start)),
            pl.BlockSpec((width, width), lambda j, *_: (j + start, 0)),
            full((SMALL, width)),
        ]
        + [left] * len(before),
        out_specs=outs + [columns, columns, full((SMALL, width)), full(kept), full(sent)],
        scratch_shapes=[pltpu.VMEM((width, width), f32)],
    )
    count = 1 + len(specs) + 5
    return pl.pallas_call(
        functools.partial(
            feed_kernel, first=first, blocks=blocks, relative=relative, tile=512
        ),
        grid_spec=grid_spec,
        out_shape=shapes
        + [
            shape((length, hidden), bf16),
            shape((length, hidden), bf16),
            shape((SMALL, width), f32),
            shape(kept, bf16),
            shape(sent, bf16),
        ],
        input_output_aliases={count + i: i for i in range(len(before))},
        compiler_params=params(),
        cost_estimate=cost(
            8 * length * width * width * blocks, 20 * length * width, 2 * length * width
        ),
        name="feed",
    )(me, *given, cot, up, upb, down, small, *before)


def finish_kernel(
    me_ref,
    act_ref,
    gh_ref,
    up_ref,
    down_ref,
    middle_ref,
    cot_ref,
    keep_ref,
    mixed_ref,
    wo_ref,
    gain_ref,
    downb_ref,
    old_ref,
    out_ref,
    gm_ref,
    gx_ref,
    small_ref,
    kept_ref,
    sent_ref,
    feed_ref,
    gn_ref,
    dw_ref,
    *,
    blocks,
    tile,
    relative,
):
    step = pl.program_id(0)

    @pl.when(step == 0)
    def _():
        small_ref[...] = old_ref[...]
        feed_ref[...] = jnp.zeros_like(feed_ref)
        gn_ref[...] = jnp.zeros_like(gn_ref)

    @pl.when(step < blocks - 1)
    def _():
        feed_ref[...] += nn(act_ref[...], down_ref[...])
        gn_ref[...] += nt(gh_ref[...], up_ref[...])

    @pl.when(step >= blocks - 1)
    def _():
        lows = []
        for i in range(tile // 256):
            here = slice(i * 256, (i + 1) * 256)
            at = pl.ds(pl.multiple_of((step - blocks + 1) * tile + i * 256, 256), 256)
            feed = feed_ref[at, :] + nn(act_ref[at, :], down_ref[...]) + downb_ref[...]
            middle = middle_ref[here, :]
            output = middle + feed
            out_ref[here, :] = output.astype(bf16)
            weight = keep_ref[here, :]
            cot = cot_ref[here, :].astype(f32)
            norm, scale = normal_rows(middle)
            grad = gn_ref[at, :] + nt(gh_ref[at, :], up_ref[...])
            inner = grad * gain_ref[...]
            grad_middle = cot + scale * (
                inner
                - jnp.mean(inner, -1, keepdims=True)
                - norm * jnp.mean(inner * norm, -1, keepdims=True)
            )
            gm_ref[here, :] = grad_middle
            low = grad_middle.astype(bf16)
            gx_ref[here, :] = nt(low, wo_ref[...]).astype(bf16)
            lows.append(low)
            small_ref[0:1, :] += jnp.sum(low.astype(f32), 0, keepdims=True)
            small_ref[1:2, :] += jnp.sum(grad * norm, 0, keepdims=True)
            small_ref[2:3, :] += jnp.sum(grad, 0, keepdims=True)
            small_ref[3:4, :] += jnp.sum(cot, 0, keepdims=True)
            small_ref[20:21, :] += jnp.sum(output * output * weight, 0, keepdims=True)
            small_ref[22:23, :] += jnp.sum(feed * feed * weight, 0, keepdims=True)
        part = tn(mixed_ref[...], jnp.concatenate(lows, 0))

        @pl.when(step == blocks - 1)
        def _():
            dw_ref[...] = part

        @pl.when(step > blocks - 1)
        def _():
            dw_ref[...] += part

    @pl.when(step == pl.num_programs(0) - 1)
    def _():
        put_rows(dw_ref, kept_ref, sent_ref, me_ref[0], relative, 0, 192, 48)


def finish_call(me, acts, up, down, middle, cot, keep, mixed, wo, gain, downb, small, relative):
    length, width = mixed.shape
    blocks = up.shape[1] // width
    end = blocks - 1
    tile = 512
    whole, row = full((length, width)), full((1, width))
    kept, sent = block_shapes(width, width, relative)
    columns = pl.BlockSpec((length, width), lambda j, *_: (0, jnp.minimum(j, end)))

    def tiled(lanes):
        return pl.BlockSpec((tile, lanes), lambda j, *_: (jnp.maximum(j - end, 0), 0))

    rows = tiled(width)
    shape = jax.ShapeDtypeStruct
    grid_spec = pltpu.PrefetchScalarGridSpec(
        num_scalar_prefetch=1,
        grid=(end + length // tile,),
        in_specs=[
            columns,
            columns,
            pl.BlockSpec((width, width), lambda j, *_: (0, jnp.minimum(j, end))),
            pl.BlockSpec((width, width), lambda j, *_: (jnp.minimum(j, end), 0)),
            rows,
            rows,
            tiled(1),
            rows,
            full((width, width)),
            row,
            row,
            full((SMALL, width)),
        ],
        out_specs=[rows, rows, rows, full((SMALL, width)), full(kept), full(sent)],
        scratch_shapes=[
            pltpu.VMEM((length, width), f32),
            pltpu.VMEM((length, width), f32),
            pltpu.VMEM((width, width), f32),
        ],
    )
    return pl.pallas_call(
        functools.partial(finish_kernel, blocks=blocks, tile=tile, relative=relative),
        grid_spec=grid_spec,
        out_shape=[
            shape((length, width), bf16),
            shape((length, width), f32),
            shape((length, width), bf16),
            shape((SMALL, width), f32),
            shape(kept, bf16),
            shape(sent, bf16),
        ],
        compiler_params=params(),
        cost_estimate=cost(4 * length * width * width, 24 * length * width),
        name="finish",
    )(me, *acts, up, down, middle, cot, keep, mixed, wo, gain, downb, small)


UNIT = 256


def units_of(part):
    each = part // UNIT
    places = [(grad, unit) for grad in range(3) for unit in range(each)]
    return [(grad, unit, i // 3, i % 3) for i, (grad, unit) in enumerate(places)]


def spread_small(small, total, chunk):
    sums = jnp.broadcast_to(jnp.sum(small[20:24, :], 1, keepdims=True), (4, chunk))
    for owner in range(16):
        lanes = slice(owner * chunk, (owner + 1) * chunk)
        block, start = owner // 4, (owner % 4) * 4 * chunk
        ups = [
            small[16 + block : 17 + block, start + i * chunk : start + (i + 1) * chunk]
            for i in range(4)
        ]
        piece = jnp.concatenate([small[0:16, lanes], *ups, sums], 0)
        high = piece.astype(bf16).astype(f32)
        whole = jnp.concatenate([high, piece - high], 0)
        for i in range(3):
            total[owner * 16 : (owner + 1) * 16, i * 128 : i * 128 + chunk] = whole[
                i * 16 : (i + 1) * 16
            ]


def weights_kernel(me_ref, n_ref, np_ref, *rest, start, count, relative):
    refs, rest = rest[: 3 * count], rest[3 * count :]
    last = count > 1
    old_ref, rest = rest[0], rest[1:]
    if last:
        x_ref, xp_ref, wq_ref, wp_ref, gq_ref, gp_ref = rest[:6]
        rest = rest[6:]
    small_ref, kept_ref, sent_ref, *totals = rest
    step = pl.program_id(0)
    grads = [ref[...] for ref in refs[-3:]]
    part = grads[0].shape[1]
    lanes = slice(start, start + part)
    sources = [n_ref[...], np_ref[...], np_ref[...]]

    @pl.when(step == 0)
    def _():
        small_ref[...] = old_ref[...]
        for total in totals[:3]:
            total[...] = jnp.zeros_like(total)

    for total, source, grad in zip(totals, sources, grads):
        total[...] += tn(source, grad)
    small_ref[4:5, lanes] += jnp.sum(grads[0].astype(f32), 0, keepdims=True)
    small_ref[7:8, lanes] += jnp.sum(grads[2].astype(f32), 0, keepdims=True)
    if last:
        dq, dk, dv = [jnp.concatenate([ref[...] for ref in refs[i::3]], 1) for i in range(3)]
        width = wq_ref.shape[0]
        far = nt(dk, wp_ref[0:2].reshape(width, width))
        far = far + nt(dv, wp_ref[2:4].reshape(width, width))
        own = nt(dq, wq_ref[...])
        gq_ref[...] = own
        gp_ref[...] = far.astype(bf16)
        norm, _ = normal_rows(x_ref[...].astype(f32))
        far_norm, _ = normal_rows(xp_ref[...].astype(f32))
        small_ref[5:6, :] += jnp.sum(own * norm, 0, keepdims=True)
        small_ref[6:7, :] += jnp.sum(own, 0, keepdims=True)
        small_ref[8:9, :] += jnp.sum(far * far_norm, 0, keepdims=True)
        small_ref[9:10, :] += jnp.sum(far, 0, keepdims=True)

    @pl.when(step == pl.num_programs(0) - 1)
    def _():
        me = me_ref[0]
        z_step = 64 if last else 48 * part // UNIT
        for grad, unit, block, place in units_of(part):
            put_rows(
                totals[grad], kept_ref, sent_ref, me, relative,
                48 * block if relative else 768 * block, 4 * z_step, z_step,
                slice(place * UNIT, (place + 1) * UNIT), slice(unit * UNIT, (unit + 1) * UNIT),
            )
        if last and relative:
            spread = totals[3]
            spread[...] = jnp.zeros_like(spread)
            spread_small(small_ref[...], spread, small_ref.shape[1] // 16)
            put_rows(spread, kept_ref, sent_ref, me, relative, 48, 4 * z_step, z_step)


def weights_call(start, me, n, n_far, grads, small, more, relative):
    length, width = n.shape
    count = len(grads) // 3
    last = count > 1
    part = grads[-1].shape[1]
    tile = 256 if last else 512
    rows = pl.BlockSpec((tile, width), lambda i, *_: (i, 0))
    extra = last and relative
    kept, sent = block_shapes(width * part // UNIT + (256 if extra else 0), width, relative)
    shape = jax.ShapeDtypeStruct
    specs = [rows, rows]
    specs += [pl.BlockSpec((tile, grad.shape[1]), lambda i, *_: (i, 0)) for grad in grads]
    specs += [full((SMALL, width))]
    outs, shapes = [], []
    if last:
        specs += [rows, rows, full(more[2].shape), full(more[3].shape)]
        outs = [rows, rows]
        shapes = [shape((length, width), f32), shape((length, width), bf16)]
    grid_spec = pltpu.PrefetchScalarGridSpec(
        num_scalar_prefetch=1,
        grid=(length // tile,),
        in_specs=specs,
        out_specs=outs + [full((SMALL, width)), full(kept), full(sent)],
        scratch_shapes=[pltpu.VMEM((width, part), f32)] * 3
        + ([pltpu.VMEM((256, width), f32)] if extra else []),
    )
    return pl.pallas_call(
        functools.partial(weights_kernel, start=start, count=count, relative=relative),
        grid_spec=grid_spec,
        out_shape=shapes
        + [shape((SMALL, width), f32), shape(kept, bf16), shape(sent, bf16)],
        compiler_params=params(),
        cost_estimate=cost(6 * length * width * part, 24 * length * width),
        name="weights",
    )(me, n, n_far, *grads, small, *more)


def tokens_kernel(x_ref, gain_ref, gm_ref, gq_ref, gf_ref, out_ref):
    norm, scale = normal_rows(x_ref[...].astype(f32))
    inner = (gq_ref[...] + gf_ref[...].astype(f32)) * gain_ref[...]
    out_ref[...] = gm_ref[...] + scale * (
        inner
        - jnp.mean(inner, -1, keepdims=True)
        - norm * jnp.mean(inner * norm, -1, keepdims=True)
    )


def tokens_call(x, gain, gm, gq, gf):
    length, width = x.shape
    rows = pl.BlockSpec((256, width), lambda i: (i, 0))
    return pl.pallas_call(
        tokens_kernel,
        grid=(length // 256,),
        in_specs=[rows, full((1, width)), rows, rows, rows],
        out_specs=rows,
        out_shape=jax.ShapeDtypeStruct((length, width), f32),
        compiler_params=params(),
        cost_estimate=cost(20 * length * width, 16 * length * width),
        name="tokens",
    )(x, gain, gm, gq, gf)


def swapped(value, axis, mask):
    pairs = [(source, source ^ mask) for source in range(lax.axis_size(axis))]
    return lax.ppermute(value, axis, pairs)


def added(a, b, dtype=bf16):
    return (a.astype(f32) + b.astype(f32)).astype(dtype)


def together(kernel, inputs, moves=(), later=(), due=()):
    count = len(moves)
    moves = list(moves) + list(later)
    inputs, values = lax.optimization_barrier((inputs, [value for value, _, _ in moves]))
    came = [swapped(value, *way[1:]) for value, way in zip(values, moves)]
    results = kernel(*inputs) if kernel else []
    results, now, due = lax.optimization_barrier((results, came[:count], list(due)))
    return results, now, came[count:], due


def total(*values):
    return functools.reduce(jnp.add, [value.astype(f32) for value in values])


def quads(*values):
    values = [value.reshape(4, -1, value.shape[-1]) for value in values]
    return jnp.concatenate(values, 1).reshape(-1, values[0].shape[-1])


def everywhere(value):
    mask = 1
    while mask < lax.axis_size("dp"):
        value = value + swapped(value, "dp", mask)
        mask *= 2
    return value


def pick_stream(pair, stream):
    return jnp.where(stream == 0, pair[0], pair[1])


def box_onehots(seg_boxes, buckets):
    half = buckets // 2
    levels = jnp.arange(buckets, dtype=jnp.int32)
    centre_x = (seg_boxes[..., 0] + seg_boxes[..., 2]) // 2
    centre_y = (seg_boxes[..., 1] + seg_boxes[..., 3]) // 2
    step_x = (
        jnp.clip((centre_x[:, None, :] - centre_x[:, :, None]) // box_step, -half, half - 1) + half
    )
    step_y = (
        jnp.clip((centre_y[:, None, :] - centre_y[:, :, None]) // box_step, -half, half - 1) + half
    )
    return (
        (step_x[..., None] == levels).astype(jnp.float32),
        (step_y[..., None] == levels).astype(jnp.float32),
    )


def body(
    tokens,
    first_gain,
    first_shift,
    query_weight,
    query_bias,
    key_weight,
    value_weight,
    value_bias,
    out_weight,
    out_bias,
    second_gain,
    second_shift,
    up_weight,
    up_bias,
    down_weight,
    down_bias,
    box_table,
    segments,
    validity,
    seg_boxes,
    cotangent,
):
    stream = lax.axis_index("stream")
    me = lax.axis_index("dp")
    shards = lax.axis_size("dp")
    width = tokens.shape[2]
    hidden = up_weight.shape[2]
    pages, page_len = segments.shape[1], segments.shape[2]
    length = pages * page_len
    relative = shards == 16
    me_ref = me.reshape(1).astype(jnp.int32)
    x = tokens[0]

    own_seg = pick_stream(segments, stream)
    far_seg = pick_stream(segments, 1 - stream)
    own_keep = pick_stream(validity, stream)
    far_keep = pick_stream(validity, 1 - stream)
    levels = jnp.arange(64, dtype=jnp.int32)
    hot_q = (own_seg[:, :, None] == levels).astype(bf16)
    hot_kt = (far_seg[:, None, :] == levels[None, :, None]).astype(bf16)
    wide_levels = jnp.arange(128, dtype=jnp.int32)
    hot_k = jnp.where(
        wide_levels == 64,
        jnp.where(far_keep[:, :, None] > 0, 0.0, mask_fill),
        (far_seg[:, :, None] == wide_levels).astype(f32),
    ).astype(bf16)
    hot_x, hot_y = box_onehots(seg_boxes, BUCKETS)
    tables = box_table[0].reshape(2, HEADS, BUCKETS)
    seg_bias = (
        jnp.einsum("pabn,hn->phab", hot_x, tables[0], precision=precise_variant)
        + jnp.einsum("pabn,hn->phab", hot_y, tables[1], precision=precise_variant)
    ).astype(bf16)
    ones = (jnp.arange(64) == 0).astype(bf16)
    seg_bias = jnp.concatenate([seg_bias, jnp.broadcast_to(ones, seg_bias.shape)], -1)

    keep_column = own_keep.reshape(length, 1).astype(f32)
    blocks, chunk = hidden // width, width // shards
    cot = cotangent[0]
    Y, CORE, X, Z1, Z2 = ("stream", 1), ("dp", 1), ("dp", 2), ("dp", 4), ("dp", 8)

    low = me & 3
    half = width // 2

    def quarter(weight):
        return lax.dynamic_slice_in_dim(weight[0], (low & 1) * half, half, 0)

    piece = jnp.where(low < 2, quarter(key_weight), quarter(value_weight))
    vectors = jnp.concatenate([first_gain, first_shift, value_bias], 0)
    (normed, query), (piece, far_rows), _, _ = together(
        query_call,
        (x, first_gain, first_shift, query_weight[0], query_bias),
        [(piece, *Y), (vectors, *Y)],
    )
    page_x = [x[page * page_len : (page + 1) * page_len] for page in range(pages)]
    (picks, hot_q, hot_k), (x_piece, core_piece, came_x), _, _ = together(
        lambda bias, hot_q, hot_k: (picks_call(hot_q, bias), hot_q, hot_k),
        (seg_bias, hot_q, hot_k),
        [(piece, *X), (piece, *CORE), (page_x[0], *Y)],
    )
    far_pages = [came_x]
    pieces = [piece, core_piece, x_piece, swapped(x_piece, *CORE)]
    far, mixing = (), ()
    for page in range(pages):

        def page_step(came, pieces, far, mixing, page=page):
            far = pair_call(page, length, me_ref, came, far_rows, pieces, far)
            return far, attend_call(page, query, far[1], far[2], picks, hot_k, mixing)

        moves = [(page_x[page + 1], *Y)] if page + 1 < pages else []
        (result, mixing), came, _, _ = together(
            page_step, (far_pages[page], pieces, tuple(far), tuple(mixing)), moves
        )
        far = result[:4]
        if page == 0:
            pieces = [result[4]]
        far_pages += came
    far_normed, keys, value_rows, far_x = far
    far_weights = pieces[0]
    mixed, log_total = mixing

    small = jnp.zeros((SMALL, width), f32)

    def feed_first(mixed, small):
        return feed_call(
            0, 2, me_ref,
            (x, mixed, keep_column, out_weight[0], out_bias, second_gain, second_shift),
            cot, up_weight[0], up_bias, down_weight[0], small, (), relative,
        )

    def feed_second(n2, small, *acts):
        return feed_call(
            1, 2, me_ref, (n2,), cot, up_weight[0], up_bias, down_weight[0], small, acts, relative
        )

    def finish(middle, small, *acts):
        return finish_call(
            me_ref, acts, up_weight[0], down_weight[0], middle, cot, keep_column, mixed,
            out_weight[0], second_gain, down_bias, small, relative,
        )

    def back_some(pair, pairs):
        def call(grad_mixed):
            return attend_back_call(
                pair, pairs, query, keys, value_rows, picks, hot_q, hot_k, hot_kt, log_total,
                mixed, grad_mixed,
            )

        return call

    def weights_some(start, more=()):
        def call(small, *grads):
            return weights_call(start, me_ref, normed, far_normed, grads, small, more, relative)

        return call

    back_through = (x, far_x, query_weight[0], far_weights)
    pairs = (4, width // 128 - 4)

    def table_row(grad_bias):
        return jnp.concatenate(
            [
                jnp.einsum("pabn,phba->hn", hot_x, grad_bias, precision=precise_variant),
                jnp.einsum("pabn,phba->hn", hot_y, grad_bias, precision=precise_variant),
            ],
            0,
        ).reshape(1, -1)

    if relative:
        z_low, z_high = (me >> 2) & 1, me >> 3

        def downs(pair):
            one, other = pair[:192], pair[192:]
            return jnp.where(z_low, other, one), jnp.where(z_low, one, other)

        (middle, normed_two, act, gh, small, ka, sa), _, _, _ = together(
            feed_first, (mixed, small)
        )
        (act, gh, small, kb, sb), (ca,), _, _ = together(
            feed_second, (normed_two, small, act, gh), [(sa, *CORE)]
        )
        up_go, down_go = added(ka[384:768], ca[384:768]), added(ka[1152:], ca[1152:])
        (output, grad_middle, grad_mixed, small, ko, so), (cb, x0, z0), _, _ = together(
            finish,
            (middle, small, act, gh),
            [(sb, *CORE), (down_go, *X), (up_go, *Z1)],
        )
        up_go = total(ka[192:384], ca[192:384], z0[192:]).astype(bf16)
        up_stay = total(ka[:192], ca[:192], z0[:192])
        go = added(kb[768:], cb[768:])
        (*grads, grad_bias), (co, z0), (x2,), _ = together(
            back_some(0, pairs[0]), (grad_mixed,), [(so, *CORE), (up_go, *Z2)], [(go, *X)]
        )
        one = total(ka[768:1152], ca[768:1152], x0).astype(bf16)
        one_keep, one_go = downs(one)
        up_low = total(up_stay, z0)
        go = jnp.concatenate([up_low[96:].astype(bf16), added(ko[192:], co[192:])], 0)
        (small, kq, sq), (z0,), (xo,), (x2,) = together(
            weights_some(0), (small, *grads), [(one_go, *Z1)], [(go, *X)], [x2]
        )
        down_one = added(one_keep, z0)
        two = total(kb[:768], cb[:768], x2).astype(bf16)
        two_keep, two_go = downs(two[384:])
        (*grads_two, grad_bias_two), (cq, z1), _, (xo,) = together(
            back_some(*pairs), (grad_mixed,), [(sq, *CORE), (two_go, *Z1)], [], [xo]
        )
        down_two = added(two_keep, z1)
        down_stay = jnp.where(z_high, down_two, down_one)
        down_go = jnp.where(z_high, down_one, down_two)
        go = added(kq[384:], cq[384:])
        rest = quads(two[:384], total(ko[:192], co[:192], xo[96:]).astype(bf16))
        (own_grad, far_grad, small, kr, sr), (xq, z1), (z3,), _ = together(
            weights_some(pairs[0] * 128, back_through),
            (small, *grads, *grads_two),
            [(go, *X), (rest[288:], *Z1)],
            [(down_go, *Z2)],
        )
        _, (cr,), (came_grad,), _ = together(None, (), [(sr, *CORE)], [(far_grad, *Y)])
        go, grad_bias, xq, z1 = lax.optimization_barrier(
            (added(kr[256:], cr[256:]), (grad_bias, grad_bias_two), xq, z1)
        )
        rest_go = added(rest[144:288], z1[144:])
        group_go = total(kq[192:384], cq[192:384], xq[192:]).astype(bf16)
        z4, z2 = swapped(group_go, *Z1), swapped(rest_go, *Z2)
        table = table_row(jnp.concatenate(grad_bias, 1))
        table = table + swapped(table, *CORE)
        _, (xr,), _, (z4, table) = together(None, (), [(go, *X)], [], [z4, table])
        r_go = total(kr[128:256], cr[128:256], xr[128:]).astype(bf16)
        group_go = total(kq[96:192], cq[96:192], xq[96:192], z4[96:]).astype(bf16)
        z5 = swapped(group_go, *Z2)
        _, (z1r, came), _, (z3,) = together(None, (), [(r_go, *Z1), (table, *X)], [], [z3])
        table = table + came
        r_go = total(kr[64:128], cr[64:128], xr[64:128], z1r[64:]).astype(bf16)
        _, (z2r, came), _, (z2, z5, came_grad) = together(
            None, (), [(r_go, *Z2), (table, *Z1)], [], [z2, z5, came_grad]
        )
        table = table + came
        up_low = total(up_low[:96], xo[:96])
        sum_down = total(down_stay, z3)
        rest = total(rest[:144], z1[:144], z2)
        first = total(kq[:96], cq[:96], xq[:96], z4[:96], z5)
        last = total(kr[:64], cr[:64], xr[:64], z1r[:64], z2r)
        sum_up = jnp.concatenate([up_low[:48], up_low[48:], rest[:48], rest[48:96]], 1)
        sum_out = rest[96:]

        def lanes_of(spread):
            pieces = [spread[:, 128 * i : 128 * i + chunk] for i in range(3)]
            pieces = jnp.concatenate(pieces, 0)
            return pieces[:SMALL] + pieces[SMALL:]

        def unit(values, place):
            block, lane = place // 3, place % 3
            return values[48 * block : 48 * block + 48, UNIT * lane : UNIT * (lane + 1)]

        def joined(first, last, i):
            return jnp.concatenate(
                [unit(first, 2 * i), unit(first, 2 * i + 1), unit(last, i)], 1
            )

        def ending(*given):
            lanes = lanes_of(last[48:])
            totals = lanes[20:24, 0]
            root_means = jnp.sqrt(totals[:3] / totals[3] + 1e-06).reshape(1, 3)
            up_part = lanes[16:20].reshape(1, hidden // shards)
            grad_tokens = tokens_call(*given)
            sum_query = joined(first, last, 0)
            return grad_tokens, lanes, root_means, up_part, sum_query, sum_up, sum_out, sum_down

        ended, (far_first, far_last, came), _, _ = together(
            ending,
            (x, first_gain, grad_middle, own_grad, came_grad),
            [(first.astype(bf16), *Y), (last, *Y), (table, *Z2)],
        )
        grad_tokens, lanes, root_means, up_part, sum_query, sum_up, sum_out, sum_down = ended
        table = table + came
        back = lanes_of(far_last[48:])[7:10]
        far_first = far_first.astype(f32)
        sum_keys, sum_values = joined(far_first, far_last, 1), joined(far_first, far_last, 2)
    else:
        middle, normed_two, act, gh, small, ka, _ = feed_first(mixed, small)
        act, gh, small, kb, _ = feed_second(normed_two, small, act, gh)
        output, grad_middle, grad_mixed, small, out_kept, _ = finish(middle, small, act, gh)
        *grads, grad_bias = back_some(0, pairs[0])(grad_mixed)
        small, kq, _ = weights_some(0)(small, *grads)
        *grads_two, grad_bias_two = back_some(*pairs)(grad_mixed)
        table = everywhere(table_row(jnp.concatenate([grad_bias, grad_bias_two], 1)))
        own_grad, far_grad, small, kr, _ = weights_some(pairs[0] * 128, back_through)(
            small, *grads, *grads_two
        )
        came_grad = swapped(far_grad, *Y)
        grad_tokens = tokens_call(x, first_gain, grad_middle, own_grad, came_grad)
        small = everywhere(small)

        def scattered(value):
            return lax.psum_scatter(value.astype(f32), "dp", scatter_dimension=0, tiled=True)

        def unit(values, place):
            block, lane = place // 3, place % 3
            return values[width * block : width * (block + 1), UNIT * lane : UNIT * (lane + 1)]

        ups = jnp.concatenate([ka, kb], 0).reshape(blocks, 2 * width, width)
        sum_up = scattered(jnp.concatenate([ups[j, :width] for j in range(blocks)], 1))
        sum_down = scattered(jnp.concatenate([ups[j, width:] for j in range(blocks)], 0))
        sum_out = scattered(out_kept)
        sum_query, sum_keys, sum_values = [
            scattered(
                jnp.concatenate([unit(kq, 2 * i), unit(kq, 2 * i + 1), unit(kr, i)], 1)
            )
            for i in range(3)
        ]
        sum_pair = jnp.concatenate([sum_keys, sum_values], 0).astype(bf16)
        lanes = lax.dynamic_slice_in_dim(small, me * chunk, chunk, 1)
        up_part = lax.dynamic_slice_in_dim(
            small[16 : 16 + blocks].reshape(1, hidden), me * (hidden // shards), hidden // shards, 1
        )
        totals = jnp.sum(small[20:24], 1)
        sum_pair, back = swapped((sum_pair, lanes[7:10]), *Y)
        root_means = jnp.sqrt(totals[:3] / totals[3] + 1e-06).reshape(1, 3)
        sum_keys, sum_values = sum_pair[:chunk].astype(f32), sum_pair[chunk:].astype(f32)

    return (
        output[None],
        grad_tokens[None],
        lanes[5:6] + back[1:2],
        lanes[6:7] + back[2:3],
        sum_query[None],
        lanes[4:5],
        sum_keys[None],
        sum_values[None],
        back[0:1],
        sum_out[None],
        lanes[0:1],
        lanes[1:2],
        lanes[2:3],
        sum_up[None],
        up_part,
        sum_down[None],
        lanes[3:4],
        lax.dynamic_slice_in_dim(table, me * chunk, chunk, 1),
        root_means,
    )


def solution(mesh):
    whole, split = P("stream", None), P("stream", "dp")
    cube, cut = P("stream", None, None), P("stream", "dp", None)
    pages = P(None, "dp", None)
    in_specs = (
        cut, whole, whole, cube, whole, cube, cube, whole, cube, whole, whole, whole,
        cube, whole, cube, whole, whole, pages, pages, P("dp", None, None), cut,
    )
    out_specs = (
        cut, cut, split, split, cut, split, cut, cut, split, cut, split, split, split,
        cut, split, cut, split, split, whole,
    )
    return jax.shard_map(body, mesh=mesh, in_specs=in_specs, out_specs=out_specs, check_vma=False)
```

profile of v0, /device:TPU:0, one launch (start us, length us, event | category | flops | bytes accessed | tf_op | source)
XLA Modules:
  0.0 281.7 jit_solution(6612461779746317990)
XLA Ops:
  1.4 1.4 select_bitcast_fusion
  2.8 3.0 %collective-permute-start = (bf16[384,768]{1,0:T(8,128)(2,1)S(1)}, bf16[384,768]{1,0:T(8,128)(2,1)S(1)}, u32[]{:S(2)}, u32[]{:S(2)}) collective-permute-start(bf16[384,768]{1,0:T(8,128)(2,1)S(1)} %select_bitcast_fusion), channel_id=1, source_target_pairs={{0,16},{16,0},{1,17},{17,1},{2,18},{18,2},{3,19},{19,3},{4,20},{20... | collective-permute-start | bytes 1769480 | tf_op jit(solution)/shard_map/ppermute | solution.py:769
  12.6 5.7 %query.1 = (bf16[1024,768]{1,0:T(8,128)(2,1)}, bf16[1024,768]{1,0:T(8,128)(2,1)}) custom-call(bf16[1024,768]{1,0:T(8,128)(2,1)} %bitcast.76, f32[1,768]{1,0:T(1,128)} %gain_ref.3, f32[1,768]{1,0:T(1,128)} %shift_ref, bf16[768,768]{1,0:T(8,128)(2,1)} %bitcast.90, f32[1,768]{1,0:T(1,128)} %b_ref), custom_call_target="tpu_custom_call" | custom-call | flops 18874368 | bytes 92160 | tf_op jit(solution)/shard_map/query/pallas_call | solution.py:71
  19.4 1.8 collective-permute-start.4
  21.2 1.5 collective-permute-start.2
  22.7 5.2 %picks.1.picks_ref = bf16[1024,1536]{1,0:T(8,128)(2,1)} custom-call(bf16[2,512,64]{2,1,0:T(8,128)(2,1)} %fusion.5.hq_ref, bf16[2,12,64,128]{3,2,1,0:T(8,128)(2,1)} %pad_maximum_fusion.3.bias_ref), custom_call_target="tpu_custom_call" | custom-call | flops 3145728 | bytes 49152 | tf_op jit(solution)/shard_map/picks/pallas_call | solution.py:158
  27.9 7.2 %collective-permute-done.2.rest_2_ = bf16[384,768]{1,0:T(8,128)(2,1)S(1)} collective-permute-done((bf16[384,768]{1,0:T(8,128)(2,1)S(1)}, bf16[384,768]{1,0:T(8,128)(2,1)S(1)}, u32[]{:S(2)}, u32[]{:S(2)}) %collective-permute-start.2) | collective-permute-done | bytes 589856 | tf_op jit(solution)/shard_map/ppermute | solution.py:769
  35.2 3.1 %collective-permute-done.4.x_ref = bf16[512,768]{1,0:T(8,128)(2,1)S(1)} collective-permute-done((bf16[512,768]{1,0:T(8,128)(2,1)S(1)}, bf16[512,768]{1,0:T(8,128)(2,1)S(1)}, u32[]{:S(2)}, u32[]{:S(2)}) %collective-permute-start.4) | collective-permute-done | bytes 786464 | tf_op jit(solution)/shard_map/ppermute | solution.py:769
  38.2 2.0 collective-permute-done.5.rest_3_
  40.2 1.4 collective-permute-start.6
  43.4 6.0 %pair.2 = (bf16[1024,768]{1,0:T(8,128)(2,1)}, bf16[1024,768]{1,0:T(8,128)(2,1)}, bf16[1024,768]{1,0:T(8,128)(2,1)}, bf16[1024,768]{1,0:T(8,128)(2,1)}, bf16[4,384,768]{2,1,0:T(8,128)(2,1)}) custom-call(s32[1]{0:T(128)} %bitcast.me_ref, bf16[512,768]{1,0:T(8,128)(2,1)} %copy-done.11, f32[3,768]{1,0:T(4,128)} %copy-done.26, bf16[384,768]{1,0:T(8,128)(2,1)} %copy-done.21, ...), custom_call_target="tpu_custom_call" | custom-call | flops 18874368 | bytes 49152 | tf_op jit(solution)/shard_map/pair/pallas_call | solution.py:133
  49.4 8.6 %attend.2 = (bf16[1024,768]{1,0:T(8,128)(2,1)}, f32[2,6,2,512]{3,2,1,0:T(2,128)}) custom-call(bf16[1024,768]{1,0:T(8,128)(2,1)} %get-tuple-element.265.q_ref, bf16[1024,768]{1,0:T(8,128)(2,1)} %get-tuple-element.282.k_ref.rest_2_, bf16[1024,768]{1,0:T(8,128)(2,1)} %get-tuple-element.283.v_ref.rest_3_, bf16[1024,1536]{1,0:T(8,128)(2,1)} %picks.1.picks_ref, ...), custom_call_target="tpu_custom_call" | custom-call | flops 50331648 | bytes 49152 | tf_op jit(solution)/shard_map/attend/pallas_call | solution.py:223
  58.0 1.8 collective-permute-done.6.x_ref
  60.7 5.2 %pair.3 = (bf16[1024,768]{1,0:T(8,128)(2,1)}, bf16[1024,768]{1,0:T(8,128)(2,1)}, bf16[1024,768]{1,0:T(8,128)(2,1)}, bf16[1024,768]{1,0:T(8,128)(2,1)}) custom-call(s32[1]{0:T(128)} %bitcast.me_ref, bf16[512,768]{1,0:T(8,128)(2,1)} %copy-done.10, f32[3,768]{1,0:T(4,128)} %copy-done.26, ...), custom_call_target="tpu_custom_call", output_to_operand_aliasing={{0}: (4, {}), {1}: (5, {}), {2}: (6, {}), {3}: (7, {})} | custom-call | flops 18874368 | bytes 49152 | tf_op jit(solution)/shard_map/pair/pallas_call | solution.py:133
  65.9 8.5 %attend.3 = (bf16[1024,768]{1,0:T(8,128)(2,1)}, f32[2,6,2,512]{3,2,1,0:T(2,128)}) custom-call(bf16[1024,768]{1,0:T(8,128)(2,1)} %get-tuple-element.265.q_ref, bf16[1024,768]{1,0:T(8,128)(2,1)} %get-tuple-element.336.k_ref, bf16[1024,768]{1,0:T(8,128)(2,1)} %get-tuple-element.337.v_ref, ...), custom_call_target="tpu_custom_call", output_to_operand_aliasing={{0}: (5, {}), {1}: (6, {})} | custom-call | flops 50331648 | bytes 49152 | tf_op jit(solution)/shard_map/attend/pallas_call | solution.py:223
  75.0 22.3 %feed.2 = (f32[1024,768]{1,0:T(8,128)}, bf16[1024,768]{1,0:T(8,128)(2,1)}, bf16[1024,3072]{1,0:T(8,128)(2,1)}, bf16[1024,3072]{1,0:T(8,128)(2,1)}, f32[24,768]{1...) custom-call(s32[1]{0:T(128)} %bitcast.me_ref, bf16[1024,768]{1,0:T(8,128)(2,1)} %bitcast.77, ...), custom_call_target="tpu_custom_call" | custom-call | flops 150994944 | bytes 245760 | tf_op jit(solution)/shard_map/feed/pallas_call | solution.py:459
  97.5 17.0 %feed.3 = (bf16[1024,3072]{1,0:T(8,128)(2,1)}, bf16[1024,3072]{1,0:T(8,128)(2,1)}, f32[24,768]{1,0:T(8,128)}, bf16[1536,768]{1,0:T(8,128)(2,1)}, bf16[1536,768]{1,0:T(8,128)(2,1)}) custom-call(s32[1]{0:T(128)} %bitcast.me_ref, bf16[1024,768]{1,0:T(8,128)(2,1)} %get-tuple-element.302.rest_0_, ...), custom_call_target="tpu_custom_call", output_to_operand_aliasing={{0}: (7, {}), {1}: (8, {})} | custom-call | flops 150994944 | bytes 245760 | tf_op jit(solution)/shard_map/feed/pallas_call | solution.py:459
  114.5 1.5 add_convert_fusion.4
  116.4 1.5 collective-permute-start.10
  117.9 1.5 collective-permute-start.9
  120.1 23.6 %finish.1 = (bf16[1024,768]{1,0:T(8,128)(2,1)}, f32[1024,768]{1,0:T(8,128)}, bf16[1024,768]{1,0:T(8,128)(2,1)}, f32[24,768]{1,0:T(8,128)}, bf16[384,768]{1,0:T(8,128)(2,1)}, /*index=5*/bf16[384,768]{1,0:T(8,128)(2,1)}) custom-call(s32[1]{0:T(128)} %bitcast.me_ref, bf16[1024,3072]{1,0:T(8,128)(2,1)} %get-tuple-element.318.act_ref, ...), custom_call_target="tpu_custom_call" | custom-call | flops 37748736 | bytes 294912 | tf_op jit(solution)/shard_map/finish/pallas_call | solution.py:605
  143.7 1.9 add_convert_fusion.12
  145.6 2.9 %add_convert_fusion.1 = bf16[768,768]{1,0:T(8,128)(2,1)} fusion(bf16[1536,768]{1,0:T(8,128)(2,1)} %collective-permute-done.8, bf16[1536,768]{1,0:T(8,128)(2,1)} %get-tuple-element.343), kind=kLoop, calls=%fused_computation.1 | loop fusion | flops 2359296 | bytes 3538944 | tf_op jit(solution)/shard_map/convert_element_type | solution.py:773
  148.5 2.6 collective-permute-start.12
  151.6 15.8 %attend_back.2 = (bf16[1024,512]{1,0:T(8,128)(2,1)}, bf16[1024,512]{1,0:T(8,128)(2,1)}, bf16[1024,512]{1,0:T(8,128)(2,1)}, f32[2,8,64,64]{3,2,1,0:T(8,128)}) custom-call(bf16[1024,768]{1,0:T(8,128)(2,1)} %get-tuple-element.265.q_ref, bf16[1024,768]{1,0:T(8,128)(2,1)} %get-tuple-element.336.k_ref, bf16[1024,768]{1,0:T(8,128)(2,1)} %get-tuple-element.337.v_ref, ...), custom_call_target="tpu_custom_call" | custom-call | flops 687194767360 | bytes 536870912 | tf_op jit(solution)/shard_map/attend_back/pallas_call | solution.py:305
  167.4 1.6 add_convert_fusion.3
  169.2 1.6 convert_add_fusion.1
  173.3 1.5 collective-permute-start.17
  174.8 7.9 %weights.2 = (f32[24,768]{1,0:T(8,128)}, bf16[768,768]{1,0:T(8,128)(2,1)}, bf16[768,768]{1,0:T(8,128)(2,1)}) custom-call(s32[1]{0:T(128)} %bitcast.me_ref, bf16[1024,768]{1,0:T(8,128)(2,1)} %get-tuple-element.333.n_ref, bf16[1024,768]{1,0:T(8,128)(2,1)} %get-tuple-element.334.np_ref, bf16[1024,512]{1,0:T(8,128)(2,1)} %get-tuple-element.387.rest_0_, ...), custom_call_target="tpu_custom_call" | custom-call | flops 37748736 | bytes 294912 | tf_op jit(solution)/shard_map/weights/pallas_call | solution.py:731
  182.8 2.1 add_convert_fusion
  186.8 1.6 collective-permute-start.16
  188.3 8.9 %attend_back.3 = (bf16[1024,256]{1,0:T(8,128)(2,1)}, bf16[1024,256]{1,0:T(8,128)(2,1)}, bf16[1024,256]{1,0:T(8,128)(2,1)}, f32[2,4,64,64]{3,2,1,0:T(8,128)}) custom-call(bf16[1024,768]{1,0:T(8,128)(2,1)} %get-tuple-element.265.q_ref, bf16[1024,768]{1,0:T(8,128)(2,1)} %get-tuple-element.336.k_ref, bf16[1024,768]{1,0:T(8,128)(2,1)} %get-tuple-element.337.v_ref, ...), custom_call_target="tpu_custom_call" | custom-call | flops 343597383680 | bytes 268435456 | tf_op jit(solution)/shard_map/attend_back/pallas_call | solution.py:305
  200.0 1.9 broadcast_select_fusion
  203.2 13.0 %weights.3 = (f32[1024,768]{1,0:T(8,128)}, bf16[1024,768]{1,0:T(8,128)(2,1)}, f32[24,768]{1,0:T(8,128)}, bf16[512,768]{1,0:T(8,128)(2,1)}, bf16[512,768]{1,0:T(8,128)(2,1)}) custom-call(s32[1]{0:T(128)} %bitcast.me_ref, bf16[1024,768]{1,0:T(8,128)(2,1)} %get-tuple-element.333.n_ref, bf16[1024,768]{1,0:T(8,128)(2,1)} %get-tuple-element.334.np_ref, ...), custom_call_target="tpu_custom_call" | custom-call | flops 18874368 | bytes 294912 | tf_op jit(solution)/shard_map/weights/pallas_call | solution.py:731
  219.5 1.5 collective-permute-start.31
  221.0 1.8 add_convert_fusion.6
  225.0 2.0 add_convert_fusion.7
  228.9 1.3 convolution_bitcast_fusion
  232.5 2.6 collective-permute-start.29
  235.1 10.2 %collective-permute-done.22 = bf16[192,768]{1,0:T(8,128)(2,1)S(1)} collective-permute-done((bf16[192,768]{1,0:T(8,128)(2,1)}, bf16[192,768]{1,0:T(8,128)(2,1)S(1)}, u32[]{:S(2)}, u32[]{:S(2)}) %collective-permute-start.22) | collective-permute-done | bytes 294944 | tf_op jit(solution)/shard_map/ppermute | solution.py:769
  248.6 1.6 collective-permute-done.25
  250.2 4.4 %collective-permute-done.24 = bf16[128,768]{1,0:T(8,128)(2,1)S(1)} collective-permute-done((bf16[128,768]{1,0:T(8,128)(2,1)S(1)}, bf16[128,768]{1,0:T(8,128)(2,1)S(1)}, u32[]{:S(2)}, u32[]{:S(2)}) %collective-permute-start.24) | collective-permute-done | bytes 196640 | tf_op jit(solution)/shard_map/ppermute | solution.py:769
  255.7 1.9 convert_add_fusion
  257.6 3.1 %collective-permute-done.30 = bf16[96,768]{1,0:T(8,128)(2,1)S(1)} collective-permute-done((bf16[96,768]{1,0:T(8,128)(2,1)S(1)}, bf16[96,768]{1,0:T(8,128)(2,1)S(1)}, u32[]{:S(2)}, u32[]{:S(2)}) %collective-permute-start.30) | collective-permute-done | bytes 147488 | tf_op jit(solution)/shard_map/ppermute | solution.py:769
  260.7 1.6 collective-permute-done.27
  266.2 1.8 collective-permute-start.33
  270.4 1.3 fusion.20
  271.7 6.6 %tokens.1 = f32[1024,768]{1,0:T(8,128)} custom-call(bf16[1024,768]{1,0:T(8,128)(2,1)} %bitcast.79, f32[1,768]{1,0:T(1,128)} %gain_ref.3, f32[1024,768]{1,0:T(8,128)} %get-tuple-element.432.gm_ref, f32[1024,768]{1,0:T(8,128)} %get-tuple-element.433.gq_ref, bf16[1024,768]{1,0:T(8,128)(2,1)} %collective-permute-done.31.gf_ref), custom_call_target="tpu_custom_call" | custom-call | flops 245760 | bytes 196608 | tf_op jit(solution)/shard_map/tokens/pallas_call | solution.py:755
  (182 shorter events, 45.1 us)
Async XLA Ops:
  0.7 5.3 %copy-start.29 = (s32[2,64,4]{1,2,0:T(4,128)S(1)}, s32[2,64,4]{1,2,0:T(4,128)}, u32[]{:S(2)}) copy-start(s32[2,64,4]{1,2,0:T(4,128)} %param.40) | copy-start | bytes 6148
  0.7 5.4 %copy-start.30 = (f32[1,768]{1,0:T(1,128)S(1)}, f32[1,768]{1,0:T(1,128)}, u32[]{:S(2)}) copy-start(f32[1,768]{1,0:T(1,128)} %param.37) | copy-start | bytes 9220
  2.8 16.6 %collective-permute-start = (bf16[384,768]{1,0:T(8,128)(2,1)S(1)}, bf16[384,768]{1,0:T(8,128)(2,1)S(1)}, u32[]{:S(2)}, u32[]{:S(2)}) collective-permute-start(bf16[384,768]{1,0:T(8,128)(2,1)S(1)} %select_bitcast_fusion), channel_id=1, source_target_pairs={{0,16},{16,0},{1,17},{17,1},{2,18},{18,2},{3,19},{19,3},{4,20},{20... | collective-permute-start | bytes 1769480 | tf_op jit(solution)/shard_map/ppermute | solution.py:769
  5.8 13.6 %collective-permute-start.1 = (f32[3,768]{1,0:T(4,128)S(1)}, f32[3,768]{1,0:T(4,128)S(1)}, u32[]{:S(2)}, u32[]{:S(2)}) collective-permute-start(f32[3,768]{1,0:T(4,128)S(1)} %pad_maximum_fusion.8), channel_id=1, source_target_pairs={{0,16},{16,0},{1,17},{17,1},{2,18},{18,2},{3,19},{19,3},{4,20},{20... | collective-permute-start | bytes 27656 | tf_op jit(solution)/shard_map/ppermute | solution.py:769
  19.4 8.5 %copy-start.26 = (f32[3,768]{1,0:T(4,128)}, f32[3,768]{1,0:T(4,128)S(1)}, u32[]{:S(2)}) copy-start(f32[3,768]{1,0:T(4,128)S(1)} %collective-permute-done.1.rows_ref) | copy-start | bytes 27652
  19.4 8.5 %copy-start.21 = (bf16[384,768]{1,0:T(8,128)(2,1)}, bf16[384,768]{1,0:T(8,128)(2,1)S(1)}, u32[]{:S(2)}) copy-start(bf16[384,768]{1,0:T(8,128)(2,1)S(1)} %collective-permute-done.rest_0_) | copy-start | bytes 1769476
  19.4 18.8 %collective-permute-start.4 = (bf16[512,768]{1,0:T(8,128)(2,1)S(1)}, bf16[512,768]{1,0:T(8,128)(2,1)S(1)}, u32[]{:S(2)}, u32[]{:S(2)}) collective-permute-start(bf16[512,768]{1,0:T(8,128)(2,1)S(1)} %get-tuple-element.250), channel_id=1, source_target_pairs={{0,16},{16,0},{1,17},{17,1},{2,18},{18,2},{3,19},{19,3},{4,20},{20... | collective-permute-start | bytes 2359304 | tf_op jit(solution)/shard_map/ppermute | solution.py:769
  21.2 13.9 %collective-permute-start.2 = (bf16[384,768]{1,0:T(8,128)(2,1)S(1)}, bf16[384,768]{1,0:T(8,128)(2,1)S(1)}, u32[]{:S(2)}, u32[]{:S(2)}) collective-permute-start(bf16[384,768]{1,0:T(8,128)(2,1)S(1)} %collective-permute-done.rest_0_), channel_id=1, source_target_pairs={{0,2},{1,3},{2,0},{3,1},{4,6},{5,7},{6,4},{7,5},{8,10},{9,11},{10,... | collective-permute-start | bytes 1769480 | tf_op jit(solution)/shard_map/ppermute | solution.py:769
  22.7 12.4 %collective-permute-start.3 = (bf16[384,768]{1,0:T(8,128)(2,1)S(1)}, bf16[384,768]{1,0:T(8,128)(2,1)}, u32[]{:S(2)}, u32[]{:S(2)}) collective-permute-start(bf16[384,768]{1,0:T(8,128)(2,1)S(1)} %collective-permute-done.rest_0_), channel_id=1, source_target_pairs={{0,1},{1,0},{2,3},{3,2},{4,5},{5,4},{6,7},{7,6},{8,9},{9,8},{10,11... | collective-permute-start | bytes 1769480 | tf_op jit(solution)/shard_map/ppermute | solution.py:769
  35.2 8.3 %copy-start.22 = (bf16[384,768]{1,0:T(8,128)(2,1)}, bf16[384,768]{1,0:T(8,128)(2,1)S(1)}, u32[]{:S(2)}) copy-start(bf16[384,768]{1,0:T(8,128)(2,1)S(1)} %collective-permute-done.2.rest_2_) | copy-start | bytes 1769476
  38.2 5.2 %copy-start.11 = (bf16[512,768]{1,0:T(8,128)(2,1)}, bf16[512,768]{1,0:T(8,128)(2,1)S(1)}, u32[]{:S(2)}) copy-start(bf16[512,768]{1,0:T(8,128)(2,1)S(1)} %collective-permute-done.4.x_ref) | copy-start | bytes 2359300
  38.2 2.0 collective-permute-start.5
  40.2 19.6 %collective-permute-start.6 = (bf16[512,768]{1,0:T(8,128)(2,1)S(1)}, bf16[512,768]{1,0:T(8,128)(2,1)S(1)}, u32[]{:S(2)}, u32[]{:S(2)}) collective-permute-start(bf16[512,768]{1,0:T(8,128)(2,1)S(1)} %get-tuple-element.270), channel_id=1, source_target_pairs={{0,16},{16,0},{1,17},{17,1},{2,18},{18,2},{3,19},{19,3},{4,20},{20... | collective-permute-start | bytes 2359304 | tf_op jit(solution)/shard_map/ppermute | solution.py:769
  97.4 17.1 %copy-start.5 = (bf16[1536,768]{1,0:T(8,128)(2,1)S(1)}, bf16[1536,768]{1,0:T(8,128)(2,1)}, u32[]{:S(2)}) copy-start(bf16[1536,768]{1,0:T(8,128)(2,1)} %get-tuple-element.316) | copy-start | bytes 7077892
  97.4 17.1 %collective-permute-start.7 = (bf16[1536,768]{1,0:T(8,128)(2,1)}, bf16[1536,768]{1,0:T(8,128)(2,1)}, u32[]{:S(2)}, u32[]{:S(2)}) collective-permute-start(bf16[1536,768]{1,0:T(8,128)(2,1)} %get-tuple-element.311), channel_id=1, source_target_pairs={{0,1},{1,0},{2,3},{3,2},{4,5},{5,4},{6,7},{7,6},{8,9},{9,8},{10,11... | collective-permute-start | bytes 7077896 | tf_op jit(solution)/shard_map/ppermute | solution.py:769
  116.0 27.7 %collective-permute-start.8 = (bf16[1536,768]{1,0:T(8,128)(2,1)}, bf16[1536,768]{1,0:T(8,128)(2,1)}, u32[]{:S(2)}, u32[]{:S(2)}) collective-permute-start(bf16[1536,768]{1,0:T(8,128)(2,1)} %get-tuple-element.328), channel_id=1, source_target_pairs={{0,1},{1,0},{2,3},{3,2},{4,5},{5,4},{6,7},{7,6},{8,9},{9,8},{10,11... | collective-permute-start | bytes 7077896 | tf_op jit(solution)/shard_map/ppermute | solution.py:769
  116.4 27.3 %collective-permute-start.10 = (bf16[384,768]{1,0:T(8,128)(2,1)S(1)}, bf16[384,768]{1,0:T(8,128)(2,1)}, u32[]{:S(2)}, u32[]{:S(2)}) collective-permute-start(bf16[384,768]{1,0:T(8,128)(2,1)S(1)} %get-tuple-element.330), channel_id=1, source_target_pairs={{0,4},{1,5},{2,6},{3,7},{4,0},{5,1},{6,2},{7,3},{8,12},{9,13},{10,... | collective-permute-start | bytes 1769480 | tf_op jit(solution)/shard_map/ppermute | solution.py:769
  117.9 25.8 %collective-permute-start.9 = (bf16[384,768]{1,0:T(8,128)(2,1)S(1)}, bf16[384,768]{1,0:T(8,128)(2,1)}, u32[]{:S(2)}, u32[]{:S(2)}) collective-permute-start(bf16[384,768]{1,0:T(8,128)(2,1)S(1)} %get-tuple-element.329), channel_id=1, source_target_pairs={{0,2},{1,3},{2,0},{3,1},{4,6},{5,7},{6,4},{7,5},{8,10},{9,11},{10,... | collective-permute-start | bytes 1769480 | tf_op jit(solution)/shard_map/ppermute | solution.py:769
  148.5 20.7 %collective-permute-start.11 = (bf16[384,768]{1,0:T(8,128)(2,1)}, bf16[384,768]{1,0:T(8,128)(2,1)}, u32[]{:S(2)}, u32[]{:S(2)}) collective-permute-start(bf16[384,768]{1,0:T(8,128)(2,1)} %get-tuple-element.350), channel_id=1, source_target_pairs={{0,1},{1,0},{2,3},{3,2},{4,5},{5,4},{6,7},{7,6},{8,9},{9,8},{10,11... | collective-permute-start | bytes 1769480 | tf_op jit(solution)/shard_map/ppermute | solution.py:769
  148.5 20.6 %collective-permute-start.12 = (bf16[192,768]{1,0:T(8,128)(2,1)}, bf16[192,768]{1,0:T(8,128)(2,1)}, u32[]{:S(2)}, u32[]{:S(2)}) collective-permute-start(bf16[192,768]{1,0:T(8,128)(2,1)} %add_convert_fusion.12), channel_id=1, source_target_pairs={{0,8},{1,9},{2,10},{3,11},{4,12},{5,13},{6,14},{7,15},{8,0},{9,1},... | collective-permute-start | bytes 884744 | tf_op jit(solution)/shard_map/ppermute | solution.py:769
  151.1 31.7 %collective-permute-start.14 = (bf16[768,768]{1,0:T(8,128)(2,1)}, bf16[768,768]{1,0:T(8,128)(2,1)}, u32[]{:S(2)}, u32[]{:S(2)}) collective-permute-start(bf16[768,768]{1,0:T(8,128)(2,1)} %add_convert_fusion.1), channel_id=1, source_target_pairs={{0,2},{1,3},{2,0},{3,1},{4,6},{5,7},{6,4},{7,5},{8,10},{9,11},{10,... | collective-permute-start | bytes 3538952 | tf_op jit(solution)/shard_map/ppermute | solution.py:769
  172.9 9.9 %collective-permute-start.13 = (bf16[192,768]{1,0:T(8,128)(2,1)S(1)}, bf16[192,768]{1,0:T(8,128)(2,1)S(1)}, u32[]{:S(2)}, u32[]{:S(2)}) collective-permute-start(bf16[192,768]{1,0:T(8,128)(2,1)S(1)} %broadcast_select_fusion.2), channel_id=1, source_target_pairs={{0,4},{1,5},{2,6},{3,7},{4,0},{5,1},{6,2},{7,3},{8,12},{9,13},{10,... | collective-permute-start | bytes 884744 | tf_op jit(solution)/shard_map/ppermute | solution.py:769
  173.3 9.5 %copy-start.6 = (bf16[1536,768]{1,0:T(8,128)(2,1)S(1)}, bf16[1536,768]{1,0:T(8,128)(2,1)}, u32[]{:S(2)}) copy-start(bf16[1536,768]{1,0:T(8,128)(2,1)} %get-tuple-element.343) | copy-start | bytes 7077892
  173.3 24.0 %collective-permute-start.17 = (bf16[288,768]{1,0:T(8,128)(2,1)}, bf16[288,768]{1,0:T(8,128)(2,1)}, u32[]{:S(2)}, u32[]{:S(2)}) collective-permute-start(bf16[288,768]{1,0:T(8,128)(2,1)} %pad_maximum_fusion.2), channel_id=1, source_target_pairs={{0,2},{1,3},{2,0},{3,1},{4,6},{5,7},{6,4},{7,5},{8,10},{9,11},{10,... | collective-permute-start | bytes 1327112 | tf_op jit(solution)/shard_map/ppermute | solution.py:769
  186.8 10.6 %collective-permute-start.15 = (bf16[768,768]{1,0:T(8,128)(2,1)}, bf16[768,768]{1,0:T(8,128)(2,1)}, u32[]{:S(2)}, u32[]{:S(2)}) collective-permute-start(bf16[768,768]{1,0:T(8,128)(2,1)} %get-tuple-element.376), channel_id=1, source_target_pairs={{0,1},{1,0},{2,3},{3,2},{4,5},{5,4},{6,7},{7,6},{8,9},{9,8},{10,11... | collective-permute-start | bytes 3538952 | tf_op jit(solution)/shard_map/ppermute | solution.py:769
  186.8 10.6 %collective-permute-start.16 = (bf16[192,768]{1,0:T(8,128)(2,1)}, bf16[192,768]{1,0:T(8,128)(2,1)}, u32[]{:S(2)}, u32[]{:S(2)}) collective-permute-start(bf16[192,768]{1,0:T(8,128)(2,1)} %broadcast_select_fusion.1), channel_id=1, source_target_pairs={{0,4},{1,5},{2,6},{3,7},{4,0},{5,1},{6,2},{7,3},{8,12},{9,13},{10,... | collective-permute-start | bytes 884744 | tf_op jit(solution)/shard_map/ppermute | solution.py:769
  188.3 8.9 %copy-start.2 = (bf16[768,768]{1,0:T(8,128)(2,1)S(1)}, bf16[768,768]{1,0:T(8,128)(2,1)}, u32[]{:S(2)}) copy-start(bf16[768,768]{1,0:T(8,128)(2,1)} %copy-done.1) | copy-start | bytes 3538948
  188.3 9.0 %copy-start.20 = (bf16[384,768]{1,0:T(8,128)(2,1)S(1)}, bf16[384,768]{1,0:T(8,128)(2,1)}, u32[]{:S(2)}) copy-start(bf16[384,768]{1,0:T(8,128)(2,1)} %get-tuple-element.357) | copy-start | bytes 1769476
  201.9 15.9 %copy-start.8 = (f32[192,768]{1,0:T(8,128)S(1)}, f32[192,768]{1,0:T(8,128)}, u32[]{:S(2)}) copy-start(f32[192,768]{1,0:T(8,128)} %copy-done.7) | copy-start | bytes 1769476
  201.9 15.6 %collective-permute-start.18 = (bf16[384,768]{1,0:T(8,128)(2,1)S(1)}, bf16[384,768]{1,0:T(8,128)(2,1)}, u32[]{:S(2)}, u32[]{:S(2)}) collective-permute-start(bf16[384,768]{1,0:T(8,128)(2,1)S(1)} %add_convert_fusion.2), channel_id=1, source_target_pairs={{0,2},{1,3},{2,0},{3,1},{4,6},{5,7},{6,4},{7,5},{8,10},{9,11},{10,... | collective-permute-start | bytes 1769480 | tf_op jit(solution)/shard_map/ppermute | solution.py:769
  202.6 13.6 %collective-permute-start.19 = (bf16[288,768]{1,0:T(8,128)(2,1)S(1)}, bf16[288,768]{1,0:T(8,128)(2,1)}, u32[]{:S(2)}, u32[]{:S(2)}) collective-permute-start(bf16[288,768]{1,0:T(8,128)(2,1)S(1)} %bitcast.98), channel_id=1, source_target_pairs={{0,4},{1,5},{2,6},{3,7},{4,0},{5,1},{6,2},{7,3},{8,12},{9,13},{10,... | collective-permute-start | bytes 1327112 | tf_op jit(solution)/shard_map/ppermute | solution.py:769
  216.3 4.7 %copy-start.12 = (bf16[512,768]{1,0:T(8,128)(2,1)S(1)}, bf16[512,768]{1,0:T(8,128)(2,1)}, u32[]{:S(2)}) copy-start(bf16[512,768]{1,0:T(8,128)(2,1)} %get-tuple-element.402) | copy-start | bytes 2359300
  217.5 3.5 %collective-permute-start.20 = (bf16[512,768]{1,0:T(8,128)(2,1)}, bf16[512,768]{1,0:T(8,128)(2,1)}, u32[]{:S(2)}, u32[]{:S(2)}) collective-permute-start(bf16[512,768]{1,0:T(8,128)(2,1)} %get-tuple-element.405), channel_id=1, source_target_pairs={{0,1},{1,0},{2,3},{3,2},{4,5},{5,4},{6,7},{7,6},{8,9},{9,8},{10,11... | collective-permute-start | bytes 2359304 | tf_op jit(solution)/shard_map/ppermute | solution.py:769
  217.5 31.0 %collective-permute-start.26 = (bf16[192,768]{1,0:T(8,128)(2,1)}, bf16[192,768]{1,0:T(8,128)(2,1)}, u32[]{:S(2)}, u32[]{:S(2)}) collective-permute-start(bf16[192,768]{1,0:T(8,128)(2,1)} %get-tuple-element.418), channel_id=1, source_target_pairs={{0,8},{1,9},{2,10},{3,11},{4,12},{5,13},{6,14},{7,15},{8,0},{9,1},... | collective-permute-start | bytes 884744 | tf_op jit(solution)/shard_map/ppermute | solution.py:769
  219.5 42.8 %collective-permute-start.31 = (bf16[1024,768]{1,0:T(8,128)(2,1)}, bf16[1024,768]{1,0:T(8,128)(2,1)}, u32[]{:S(2)}, u32[]{:S(2)}) collective-permute-start(bf16[1024,768]{1,0:T(8,128)(2,1)} %get-tuple-element.425), channel_id=1, source_target_pairs={{0,16},{16,0},{1,17},{17,1},{2,18},{18,2},{3,19},{19,3},{4,20},{20... | collective-permute-start | bytes 4718600 | tf_op jit(solution)/shard_map/ppermute | solution.py:769
  227.0 18.4 %copy-start.13 = (bf16[512,768]{1,0:T(8,128)(2,1)S(1)}, bf16[512,768]{1,0:T(8,128)(2,1)}, u32[]{:S(2)}) copy-start(bf16[512,768]{1,0:T(8,128)(2,1)} %get-tuple-element.402) | copy-start | bytes 2359300
  227.0 18.4 %collective-permute-start.21 = (bf16[256,768]{1,0:T(8,128)(2,1)}, bf16[256,768]{1,0:T(8,128)(2,1)}, u32[]{:S(2)}, u32[]{:S(2)}) collective-permute-start(bf16[256,768]{1,0:T(8,128)(2,1)} %add_convert_fusion.6), channel_id=1, source_target_pairs={{0,2},{1,3},{2,0},{3,1},{4,6},{5,7},{6,4},{7,5},{8,10},{9,11},{10,... | collective-permute-start | bytes 1179656 | tf_op jit(solution)/shard_map/ppermute | solution.py:769
  230.2 15.1 %collective-permute-start.22 = (bf16[192,768]{1,0:T(8,128)(2,1)}, bf16[192,768]{1,0:T(8,128)(2,1)S(1)}, u32[]{:S(2)}, u32[]{:S(2)}) collective-permute-start(bf16[192,768]{1,0:T(8,128)(2,1)} %add_convert_fusion.7), channel_id=1, source_target_pairs={{0,4},{1,5},{2,6},{3,7},{4,0},{5,1},{6,2},{7,3},{8,12},{9,13},{10,... | collective-permute-start | bytes 884744 | tf_op jit(solution)/shard_map/ppermute | solution.py:769
  231.3 1.2 collective-permute-start.23
  232.5 25.1 %collective-permute-start.29 = (bf16[144,768]{1,0:T(8,128)(2,1)S(1)}, bf16[144,768]{1,0:T(8,128)(2,1)S(1)}, u32[]{:S(2)}, u32[]{:S(2)}) collective-permute-start(bf16[144,768]{1,0:T(8,128)(2,1)S(1)} %fusion.8), channel_id=1, source_target_pairs={{0,8},{1,9},{2,10},{3,11},{4,12},{5,13},{6,14},{7,15},{8,0},{9,1},... | collective-permute-start | bytes 663560 | tf_op jit(solution)/shard_map/ppermute | solution.py:769
  246.4 8.2 %collective-permute-start.24 = (bf16[128,768]{1,0:T(8,128)(2,1)S(1)}, bf16[128,768]{1,0:T(8,128)(2,1)S(1)}, u32[]{:S(2)}, u32[]{:S(2)}) collective-permute-start(bf16[128,768]{1,0:T(8,128)(2,1)S(1)} %add_convert_fusion.13), channel_id=1, source_target_pairs={{0,4},{1,5},{2,6},{3,7},{4,0},{5,1},{6,2},{7,3},{8,12},{9,13},{10,... | collective-permute-start | bytes 589832 | tf_op jit(solution)/shard_map/ppermute | solution.py:769
  246.5 3.7 %collective-permute-start.25 = (f32[1,768]{1,0:T(1,128)S(1)}, f32[1,768]{1,0:T(1,128)S(1)}, u32[]{:S(2)}, u32[]{:S(2)}) collective-permute-start(f32[1,768]{1,0:T(1,128)S(1)} %add.260), channel_id=1, source_target_pairs={{0,2},{1,3},{2,0},{3,1},{4,6},{5,7},{6,4},{7,5},{8,10},{9,11},{10,... | collective-permute-start | bytes 9224 | tf_op jit(solution)/shard_map/ppermute | solution.py:769
  248.5 12.2 %collective-permute-start.30 = (bf16[96,768]{1,0:T(8,128)(2,1)S(1)}, bf16[96,768]{1,0:T(8,128)(2,1)S(1)}, u32[]{:S(2)}, u32[]{:S(2)}) collective-permute-start(bf16[96,768]{1,0:T(8,128)(2,1)S(1)} %add_convert_fusion.14), channel_id=1, source_target_pairs={{0,8},{1,9},{2,10},{3,11},{4,12},{5,13},{6,14},{7,15},{8,0},{9,1},... | collective-permute-start | bytes 442376 | tf_op jit(solution)/shard_map/ppermute | solution.py:769
  255.6 6.7 %collective-permute-start.27 = (bf16[64,768]{1,0:T(8,128)(2,1)S(1)}, bf16[64,768]{1,0:T(8,128)(2,1)S(1)}, u32[]{:S(2)}, u32[]{:S(2)}) collective-permute-start(bf16[64,768]{1,0:T(8,128)(2,1)S(1)} %add_convert_fusion.15), channel_id=1, source_target_pairs={{0,8},{1,9},{2,10},{3,11},{4,12},{5,13},{6,14},{7,15},{8,0},{9,1},... | collective-permute-start | bytes 294920 | tf_op jit(solution)/shard_map/ppermute | solution.py:769
  255.6 5.0 %collective-permute-start.28 = (f32[1,768]{1,0:T(1,128)S(1)}, f32[1,768]{1,0:T(1,128)S(1)}, u32[]{:S(2)}, u32[]{:S(2)}) collective-permute-start(f32[1,768]{1,0:T(1,128)S(1)} %add.265), channel_id=1, source_target_pairs={{0,4},{1,5},{2,6},{3,7},{4,0},{5,1},{6,2},{7,3},{8,12},{9,13},{10,... | collective-permute-start | bytes 9224 | tf_op jit(solution)/shard_map/ppermute | solution.py:769
  266.2 12.7 %collective-permute-start.33 = (f32[64,768]{1,0:T(8,128)S(1)}, f32[64,768]{1,0:T(8,128)S(1)}, u32[]{:S(2)}, u32[]{:S(2)}) collective-permute-start(f32[64,768]{1,0:T(8,128)S(1)} %convert_add_fusion.5), channel_id=1, source_target_pairs={{0,16},{16,0},{1,17},{17,1},{2,18},{18,2},{3,19},{19,3},{4,20},{20... | collective-permute-start | bytes 589832 | tf_op jit(solution)/shard_map/ppermute | solution.py:769
  268.0 10.9 %collective-permute-start.32 = (bf16[96,768]{1,0:T(8,128)(2,1)S(1)}, bf16[96,768]{1,0:T(8,128)(2,1)S(1)}, u32[]{:S(2)}, u32[]{:S(2)}) collective-permute-start(bf16[96,768]{1,0:T(8,128)(2,1)S(1)} %get-tuple-element.437), channel_id=1, source_target_pairs={{0,16},{16,0},{1,17},{17,1},{2,18},{18,2},{3,19},{19,3},{4,20},{20... | collective-permute-start | bytes 442376 | tf_op jit(solution)/shard_map/ppermute | solution.py:769
  268.3 10.6 %collective-permute-start.34 = (f32[1,768]{1,0:T(1,128)S(1)}, f32[1,768]{1,0:T(1,128)S(1)}, u32[]{:S(2)}, u32[]{:S(2)}) collective-permute-start(f32[1,768]{1,0:T(1,128)S(1)} %add.278), channel_id=1, source_target_pairs={{0,8},{1,9},{2,10},{3,11},{4,12},{5,13},{6,14},{7,15},{8,0},{9,1},... | collective-permute-start | bytes 9224 | tf_op jit(solution)/shard_map/ppermute | solution.py:769
  (18 other events, 37.7 us)
where the time goes:
time: 286 us; the launch traced here: 282 us
  Pallas kernels  154 us (54%)
  other arithmetic  46.9 us (16%)
  waiting for transfers between devices  37.6 us (13%)
  starting transfers between devices  28.6 us (10%)
  local copies, waits for them, and re-layouts  8.59 us (3%)
  matrix products  4.07 us (1%)
    pallas_call x2, Pallas kernels, feed_call(): pl.pallas_call(functools.partial(feed_kernel, first=first, blocks=blocks,...  39.4 us
    ppermute x35, waiting for transfers between devices, swapped(): return lax.ppermute(value, axis, pairs)  37.6 us
    ppermute x35, starting transfers between devices, swapped(): return lax.ppermute(value, axis, pairs)  28.6 us
    pallas_call x2, Pallas kernels, attend_back_call(): pl.pallas_call(attend_back_kernel, grid=(pages, pairs // PAIRS), in_specs...  24.7 us
    pallas_call x1, Pallas kernels, finish_call(): pl.pallas_call(functools.partial(finish_kernel, blocks=blocks, tile=tile,...  23.6 us
    pallas_call x2, Pallas kernels, weights_call(): pl.pallas_call(functools.partial(weights_kernel, start=start, count=count...  21 us
    pallas_call x2, Pallas kernels, attend_call(): pl.pallas_call(attend_kernel, grid=(1, width // 128 // PAIRS), in_specs=[...  17 us
    pallas_call x2, Pallas kernels, pair_call(): pl.pallas_call(functools.partial(pair_kernel, count=len(pieces)), grid_sp...  11.2 us
  transfers between devices with their start and end apart: 35, of which 12 were waited for; matrix products, arithmetic and copies ran while one was open for 13% of the time, Pallas kernels for 42%

commit v1 on v0

--- a/solution.py
+++ b/solution.py
@@ -516,8 +516,11 @@
 
     @pl.when(step < blocks - 1)
     def _():
-        feed_ref[...] += nn(act_ref[...], down_ref[...])
-        gn_ref[...] += nt(gh_ref[...], up_ref[...])
+        @pl.loop(0, feed_ref.shape[0] // 512)
+        def _(i):
+            at = pl.ds(pl.multiple_of(i * 512, 512), 512)
+            feed_ref[at, :] += nn(act_ref[at, :], down_ref[...])
+            gn_ref[at, :] += nt(gh_ref[at, :], up_ref[...])
 
     @pl.when(step >= blocks - 1)
     def _():
@@ -890,10 +893,12 @@
 
     piece = jnp.where(low < 2, quarter(key_weight), quarter(value_weight))
     vectors = jnp.concatenate([first_gain, first_shift, value_bias], 0)
-    (normed, query), (piece, far_rows), _, _ = together(
+    (normed, query), (piece,), _, (far_rows,) = together(
         query_call,
         (x, first_gain, first_shift, query_weight[0], query_bias),
-        [(piece, *Y), (vectors, *Y)],
+        [(piece, *Y)],
+        [],
+        [swapped(vectors, *Y)],
     )
     page_x = [x[page * page_len : (page + 1) * page_len] for page in range(pages)]
     (picks, hot_q, hot_k), (x_piece, core_piece, came_x), _, _ = together(

time: 286 us -> 286 us (level)
  no operation moved by 1% of the time
where the time goes in v1:
time: 286 us; the launch traced here: 281 us
  Pallas kernels  155 us (54%)
  other arithmetic  46.2 us (16%)
  waiting for transfers between devices  35.8 us (13%)
  starting transfers between devices  29.9 us (10%)
  local copies, waits for them, and re-layouts  8.6 us (3%)
  matrix products  4.07 us (1%)
    pallas_call x2, Pallas kernels, feed_call(): pl.pallas_call(functools.partial(feed_kernel, first=first, blocks=blocks,...  39.3 us
    ppermute x35, waiting for transfers between devices, swapped(): return lax.ppermute(value, axis, pairs)  35.8 us
    ppermute x35, starting transfers between devices, swapped(): return lax.ppermute(value, axis, pairs)  29.9 us
    pallas_call x2, Pallas kernels, attend_back_call(): pl.pallas_call(attend_back_kernel, grid=(pages, pairs // PAIRS), in_specs...  24.5 us
    pallas_call x1, Pallas kernels, finish_call(): pl.pallas_call(functools.partial(finish_kernel, blocks=blocks, tile=tile,...  24.1 us
    pallas_call x2, Pallas kernels, weights_call(): pl.pallas_call(functools.partial(weights_kernel, start=start, count=count...  21 us
    pallas_call x2, Pallas kernels, attend_call(): pl.pallas_call(attend_kernel, grid=(1, width // 128 // PAIRS), in_specs=[...  17.1 us
    pallas_call x2, Pallas kernels, pair_call(): pl.pallas_call(functools.partial(pair_kernel, count=len(pieces)), grid_sp...  11.2 us
  transfers between devices with their start and end apart: 35, of which 12 were waited for; matrix products, arithmetic and copies ran while one was open for 13% of the time, Pallas kernels for 42%

profile of v1, /device:TPU:0, one launch (start us, length us, event | category | flops | bytes accessed | tf_op | source)
XLA Modules:
  0.0 281.3 jit_solution(13504162020573028304)
XLA Ops:
  0.7 1.4 select_bitcast_fusion
  2.1 3.0 %collective-permute-start = (bf16[384,768]{1,0:T(8,128)(2,1)S(1)}, bf16[384,768]{1,0:T(8,128)(2,1)S(1)}, u32[]{:S(2)}, u32[]{:S(2)}) collective-permute-start(bf16[384,768]{1,0:T(8,128)(2,1)S(1)} %select_bitcast_fusion), channel_id=1, source_target_pairs={{0,16},{16,0},{1,17},{17,1},{2,18},{18,2},{3,19},{19,3},{4,20},{20... | collective-permute-start | bytes 1769480 | tf_op jit(solution)/shard_map/ppermute | solution.py:772
  12.0 6.0 %query.1 = (bf16[1024,768]{1,0:T(8,128)(2,1)}, bf16[1024,768]{1,0:T(8,128)(2,1)}) custom-call(bf16[1024,768]{1,0:T(8,128)(2,1)} %bitcast.76, f32[1,768]{1,0:T(1,128)} %gain_ref.3, f32[1,768]{1,0:T(1,128)} %shift_ref, bf16[768,768]{1,0:T(8,128)(2,1)} %bitcast.90, f32[1,768]{1,0:T(1,128)} %b_ref), custom_call_target="tpu_custom_call" | custom-call | flops 18874368 | bytes 92160 | tf_op jit(solution)/shard_map/query/pallas_call | solution.py:71
  18.8 1.8 collective-permute-start.4
  20.6 1.5 collective-permute-start.2
  22.0 5.2 %picks.1.picks_ref = bf16[1024,1536]{1,0:T(8,128)(2,1)} custom-call(bf16[2,512,64]{2,1,0:T(8,128)(2,1)} %fusion.5.hq_ref, bf16[2,12,64,128]{3,2,1,0:T(8,128)(2,1)} %pad_maximum_fusion.3.bias_ref), custom_call_target="tpu_custom_call" | custom-call | flops 3145728 | bytes 49152 | tf_op jit(solution)/shard_map/picks/pallas_call | solution.py:158
  27.2 7.2 %collective-permute-done.2.rest_2_ = bf16[384,768]{1,0:T(8,128)(2,1)S(1)} collective-permute-done((bf16[384,768]{1,0:T(8,128)(2,1)S(1)}, bf16[384,768]{1,0:T(8,128)(2,1)S(1)}, u32[]{:S(2)}, u32[]{:S(2)}) %collective-permute-start.2) | collective-permute-done | bytes 589856 | tf_op jit(solution)/shard_map/ppermute | solution.py:772
  34.5 3.1 %collective-permute-done.4.x_ref = bf16[512,768]{1,0:T(8,128)(2,1)S(1)} collective-permute-done((bf16[512,768]{1,0:T(8,128)(2,1)S(1)}, bf16[512,768]{1,0:T(8,128)(2,1)S(1)}, u32[]{:S(2)}, u32[]{:S(2)}) %collective-permute-start.4) | collective-permute-done | bytes 786464 | tf_op jit(solution)/shard_map/ppermute | solution.py:772
  37.5 2.0 collective-permute-done.5.rest_3_
  39.5 1.4 collective-permute-start.6
  42.7 6.0 %pair.2 = (bf16[1024,768]{1,0:T(8,128)(2,1)}, bf16[1024,768]{1,0:T(8,128)(2,1)}, bf16[1024,768]{1,0:T(8,128)(2,1)}, bf16[1024,768]{1,0:T(8,128)(2,1)}, bf16[4,384,768]{2,1,0:T(8,128)(2,1)}) custom-call(s32[1]{0:T(128)} %bitcast.me_ref, bf16[512,768]{1,0:T(8,128)(2,1)} %copy-done.11, f32[3,768]{1,0:T(4,128)} %copy-done.26, bf16[384,768]{1,0:T(8,128)(2,1)} %copy-done.21, ...), custom_call_target="tpu_custom_call" | custom-call | flops 18874368 | bytes 49152 | tf_op jit(solution)/shard_map/pair/pallas_call | solution.py:133
  48.7 8.6 %attend.2 = (bf16[1024,768]{1,0:T(8,128)(2,1)}, f32[2,6,2,512]{3,2,1,0:T(2,128)}) custom-call(bf16[1024,768]{1,0:T(8,128)(2,1)} %get-tuple-element.263.q_ref, bf16[1024,768]{1,0:T(8,128)(2,1)} %get-tuple-element.280.k_ref.rest_2_, bf16[1024,768]{1,0:T(8,128)(2,1)} %get-tuple-element.281.v_ref.rest_3_, bf16[1024,1536]{1,0:T(8,128)(2,1)} %picks.1.picks_ref, ...), custom_call_target="tpu_custom_call" | custom-call | flops 50331648 | bytes 49152 | tf_op jit(solution)/shard_map/attend/pallas_call | solution.py:223
  57.3 1.9 collective-permute-done.6.x_ref
  60.0 5.2 %pair.3 = (bf16[1024,768]{1,0:T(8,128)(2,1)}, bf16[1024,768]{1,0:T(8,128)(2,1)}, bf16[1024,768]{1,0:T(8,128)(2,1)}, bf16[1024,768]{1,0:T(8,128)(2,1)}) custom-call(s32[1]{0:T(128)} %bitcast.me_ref, bf16[512,768]{1,0:T(8,128)(2,1)} %copy-done.10, f32[3,768]{1,0:T(4,128)} %copy-done.26, ...), custom_call_target="tpu_custom_call", output_to_operand_aliasing={{0}: (4, {}), {1}: (5, {}), {2}: (6, {}), {3}: (7, {})} | custom-call | flops 18874368 | bytes 49152 | tf_op jit(solution)/shard_map/pair/pallas_call | solution.py:133
  65.2 8.5 %attend.3 = (bf16[1024,768]{1,0:T(8,128)(2,1)}, f32[2,6,2,512]{3,2,1,0:T(2,128)}) custom-call(bf16[1024,768]{1,0:T(8,128)(2,1)} %get-tuple-element.263.q_ref, bf16[1024,768]{1,0:T(8,128)(2,1)} %get-tuple-element.334.k_ref, bf16[1024,768]{1,0:T(8,128)(2,1)} %get-tuple-element.335.v_ref, ...), custom_call_target="tpu_custom_call", output_to_operand_aliasing={{0}: (5, {}), {1}: (6, {})} | custom-call | flops 50331648 | bytes 49152 | tf_op jit(solution)/shard_map/attend/pallas_call | solution.py:223
  74.3 22.4 %feed.2 = (f32[1024,768]{1,0:T(8,128)}, bf16[1024,768]{1,0:T(8,128)(2,1)}, bf16[1024,3072]{1,0:T(8,128)(2,1)}, bf16[1024,3072]{1,0:T(8,128)(2,1)}, f32[24,768]{1...) custom-call(s32[1]{0:T(128)} %bitcast.me_ref, bf16[1024,768]{1,0:T(8,128)(2,1)} %bitcast.77, ...), custom_call_target="tpu_custom_call" | custom-call | flops 150994944 | bytes 245760 | tf_op jit(solution)/shard_map/feed/pallas_call | solution.py:459
  96.8 17.0 %feed.3 = (bf16[1024,3072]{1,0:T(8,128)(2,1)}, bf16[1024,3072]{1,0:T(8,128)(2,1)}, f32[24,768]{1,0:T(8,128)}, bf16[1536,768]{1,0:T(8,128)(2,1)}, bf16[1536,768]{1,0:T(8,128)(2,1)}) custom-call(s32[1]{0:T(128)} %bitcast.me_ref, bf16[1024,768]{1,0:T(8,128)(2,1)} %get-tuple-element.300.rest_0_, ...), custom_call_target="tpu_custom_call", output_to_operand_aliasing={{0}: (7, {}), {1}: (8, {})} | custom-call | flops 150994944 | bytes 245760 | tf_op jit(solution)/shard_map/feed/pallas_call | solution.py:459
  113.8 1.5 add_convert_fusion.4
  115.7 1.5 collective-permute-start.10
  117.2 1.5 collective-permute-start.9
  119.3 24.1 %finish.1 = (bf16[1024,768]{1,0:T(8,128)(2,1)}, f32[1024,768]{1,0:T(8,128)}, bf16[1024,768]{1,0:T(8,128)(2,1)}, f32[24,768]{1,0:T(8,128)}, bf16[384,768]{1,0:T(8,128)(2,1)}, /*index=5*/bf16[384,768]{1,0:T(8,128)(2,1)}) custom-call(s32[1]{0:T(128)} %bitcast.me_ref, bf16[1024,3072]{1,0:T(8,128)(2,1)} %get-tuple-element.316.act_ref, ...), custom_call_target="tpu_custom_call" | custom-call | flops 37748736 | bytes 294912 | tf_op jit(solution)/shard_map/finish/pallas_call | solution.py:608
  143.5 1.9 add_convert_fusion.12
  145.3 2.9 %add_convert_fusion.1 = bf16[768,768]{1,0:T(8,128)(2,1)} fusion(bf16[1536,768]{1,0:T(8,128)(2,1)} %collective-permute-done.8, bf16[1536,768]{1,0:T(8,128)(2,1)} %get-tuple-element.341), kind=kLoop, calls=%fused_computation.1 | loop fusion | flops 2359296 | bytes 3538944 | tf_op jit(solution)/shard_map/convert_element_type | solution.py:776
  148.3 2.6 collective-permute-start.12
  151.4 15.6 %attend_back.2 = (bf16[1024,512]{1,0:T(8,128)(2,1)}, bf16[1024,512]{1,0:T(8,128)(2,1)}, bf16[1024,512]{1,0:T(8,128)(2,1)}, f32[2,8,64,64]{3,2,1,0:T(8,128)}) custom-call(bf16[1024,768]{1,0:T(8,128)(2,1)} %get-tuple-element.263.q_ref, bf16[1024,768]{1,0:T(8,128)(2,1)} %get-tuple-element.334.k_ref, bf16[1024,768]{1,0:T(8,128)(2,1)} %get-tuple-element.335.v_ref, ...), custom_call_target="tpu_custom_call" | custom-call | flops 687194767360 | bytes 536870912 | tf_op jit(solution)/shard_map/attend_back/pallas_call | solution.py:305
  167.0 1.6 add_convert_fusion.3
  168.7 1.6 convert_add_fusion.1
  172.9 1.5 collective-permute-start.17
  174.4 7.9 %weights.2 = (f32[24,768]{1,0:T(8,128)}, bf16[768,768]{1,0:T(8,128)(2,1)}, bf16[768,768]{1,0:T(8,128)(2,1)}) custom-call(s32[1]{0:T(128)} %bitcast.me_ref, bf16[1024,768]{1,0:T(8,128)(2,1)} %get-tuple-element.331.n_ref, bf16[1024,768]{1,0:T(8,128)(2,1)} %get-tuple-element.332.np_ref, bf16[1024,512]{1,0:T(8,128)(2,1)} %get-tuple-element.385.rest_0_, ...), custom_call_target="tpu_custom_call" | custom-call | flops 37748736 | bytes 294912 | tf_op jit(solution)/shard_map/weights/pallas_call | solution.py:734
  182.4 2.1 add_convert_fusion
  186.3 1.6 collective-permute-start.16
  187.9 8.9 %attend_back.3 = (bf16[1024,256]{1,0:T(8,128)(2,1)}, bf16[1024,256]{1,0:T(8,128)(2,1)}, bf16[1024,256]{1,0:T(8,128)(2,1)}, f32[2,4,64,64]{3,2,1,0:T(8,128)}) custom-call(bf16[1024,768]{1,0:T(8,128)(2,1)} %get-tuple-element.263.q_ref, bf16[1024,768]{1,0:T(8,128)(2,1)} %get-tuple-element.334.k_ref, bf16[1024,768]{1,0:T(8,128)(2,1)} %get-tuple-element.335.v_ref, ...), custom_call_target="tpu_custom_call" | custom-call | flops 343597383680 | bytes 268435456 | tf_op jit(solution)/shard_map/attend_back/pallas_call | solution.py:305
  199.6 1.9 broadcast_select_fusion
  202.8 13.1 %weights.3 = (f32[1024,768]{1,0:T(8,128)}, bf16[1024,768]{1,0:T(8,128)(2,1)}, f32[24,768]{1,0:T(8,128)}, bf16[512,768]{1,0:T(8,128)(2,1)}, bf16[512,768]{1,0:T(8,128)(2,1)}) custom-call(s32[1]{0:T(128)} %bitcast.me_ref, bf16[1024,768]{1,0:T(8,128)(2,1)} %get-tuple-element.331.n_ref, bf16[1024,768]{1,0:T(8,128)(2,1)} %get-tuple-element.332.np_ref, ...), custom_call_target="tpu_custom_call" | custom-call | flops 18874368 | bytes 294912 | tf_op jit(solution)/shard_map/weights/pallas_call | solution.py:734
  219.0 1.5 collective-permute-start.31
  220.5 1.8 add_convert_fusion.6
  224.5 2.0 add_convert_fusion.7
  228.5 1.3 convolution_bitcast_fusion
  232.1 2.6 collective-permute-start.29
  234.7 10.0 %collective-permute-done.22 = bf16[192,768]{1,0:T(8,128)(2,1)S(1)} collective-permute-done((bf16[192,768]{1,0:T(8,128)(2,1)}, bf16[192,768]{1,0:T(8,128)(2,1)S(1)}, u32[]{:S(2)}, u32[]{:S(2)}) %collective-permute-start.22) | collective-permute-done | bytes 294944 | tf_op jit(solution)/shard_map/ppermute | solution.py:772
  248.1 1.4 collective-permute-done.25
  249.6 4.4 %collective-permute-done.24 = bf16[128,768]{1,0:T(8,128)(2,1)S(1)} collective-permute-done((bf16[128,768]{1,0:T(8,128)(2,1)S(1)}, bf16[128,768]{1,0:T(8,128)(2,1)S(1)}, u32[]{:S(2)}, u32[]{:S(2)}) %collective-permute-start.24) | collective-permute-done | bytes 196640 | tf_op jit(solution)/shard_map/ppermute | solution.py:772
  256.2 1.9 convert_add_fusion
  258.1 2.2 collective-permute-done.30
  260.3 1.5 collective-permute-done.27
  265.7 1.8 collective-permute-start.33
  269.9 1.3 fusion.20
  271.2 6.6 %tokens.1 = f32[1024,768]{1,0:T(8,128)} custom-call(bf16[1024,768]{1,0:T(8,128)(2,1)} %bitcast.79, f32[1,768]{1,0:T(1,128)} %gain_ref.3, f32[1024,768]{1,0:T(8,128)} %get-tuple-element.430.gm_ref, f32[1024,768]{1,0:T(8,128)} %get-tuple-element.431.gq_ref, bf16[1024,768]{1,0:T(8,128)(2,1)} %collective-permute-done.31.gf_ref), custom_call_target="tpu_custom_call" | custom-call | flops 245760 | bytes 196608 | tf_op jit(solution)/shard_map/tokens/pallas_call | solution.py:758
  (188 shorter events, 45.3 us)
Async XLA Ops:
  0.7 4.7 %copy-start.32 = (f32[1,768]{1,0:T(1,128)S(1)}, f32[1,768]{1,0:T(1,128)}, u32[]{:S(2)}) copy-start(f32[1,768]{1,0:T(1,128)} %param.37) | copy-start | bytes 9220
  2.1 16.6 %collective-permute-start = (bf16[384,768]{1,0:T(8,128)(2,1)S(1)}, bf16[384,768]{1,0:T(8,128)(2,1)S(1)}, u32[]{:S(2)}, u32[]{:S(2)}) collective-permute-start(bf16[384,768]{1,0:T(8,128)(2,1)S(1)} %select_bitcast_fusion), channel_id=1, source_target_pairs={{0,16},{16,0},{1,17},{17,1},{2,18},{18,2},{3,19},{19,3},{4,20},{20... | collective-permute-start | bytes 1769480 | tf_op jit(solution)/shard_map/ppermute | solution.py:772
  5.2 13.6 %collective-permute-start.1 = (f32[3,768]{1,0:T(4,128)S(1)}, f32[3,768]{1,0:T(4,128)S(1)}, u32[]{:S(2)}, u32[]{:S(2)}) collective-permute-start(f32[3,768]{1,0:T(4,128)S(1)} %pad_maximum_fusion.8), channel_id=1, source_target_pairs={{0,16},{16,0},{1,17},{17,1},{2,18},{18,2},{3,19},{19,3},{4,20},{20... | collective-permute-start | bytes 27656 | tf_op jit(solution)/shard_map/ppermute | solution.py:772
  18.7 8.5 %copy-start.26 = (f32[3,768]{1,0:T(4,128)}, f32[3,768]{1,0:T(4,128)S(1)}, u32[]{:S(2)}) copy-start(f32[3,768]{1,0:T(4,128)S(1)} %collective-permute-done.1.rows_ref) | copy-start | bytes 27652
  18.7 8.5 %copy-start.21 = (bf16[384,768]{1,0:T(8,128)(2,1)}, bf16[384,768]{1,0:T(8,128)(2,1)S(1)}, u32[]{:S(2)}) copy-start(bf16[384,768]{1,0:T(8,128)(2,1)S(1)} %collective-permute-done.rest_0_) | copy-start | bytes 1769476
  18.8 18.8 %collective-permute-start.4 = (bf16[512,768]{1,0:T(8,128)(2,1)S(1)}, bf16[512,768]{1,0:T(8,128)(2,1)S(1)}, u32[]{:S(2)}, u32[]{:S(2)}) collective-permute-start(bf16[512,768]{1,0:T(8,128)(2,1)S(1)} %get-tuple-element.248), channel_id=1, source_target_pairs={{0,16},{16,0},{1,17},{17,1},{2,18},{18,2},{3,19},{19,3},{4,20},{20... | collective-permute-start | bytes 2359304 | tf_op jit(solution)/shard_map/ppermute | solution.py:772
  20.6 13.9 %collective-permute-start.2 = (bf16[384,768]{1,0:T(8,128)(2,1)S(1)}, bf16[384,768]{1,0:T(8,128)(2,1)S(1)}, u32[]{:S(2)}, u32[]{:S(2)}) collective-permute-start(bf16[384,768]{1,0:T(8,128)(2,1)S(1)} %collective-permute-done.rest_0_), channel_id=1, source_target_pairs={{0,2},{1,3},{2,0},{3,1},{4,6},{5,7},{6,4},{7,5},{8,10},{9,11},{10,... | collective-permute-start | bytes 1769480 | tf_op jit(solution)/shard_map/ppermute | solution.py:772
  22.0 12.4 %collective-permute-start.3 = (bf16[384,768]{1,0:T(8,128)(2,1)S(1)}, bf16[384,768]{1,0:T(8,128)(2,1)}, u32[]{:S(2)}, u32[]{:S(2)}) collective-permute-start(bf16[384,768]{1,0:T(8,128)(2,1)S(1)} %collective-permute-done.rest_0_), channel_id=1, source_target_pairs={{0,1},{1,0},{2,3},{3,2},{4,5},{5,4},{6,7},{7,6},{8,9},{9,8},{10,11... | collective-permute-start | bytes 1769480 | tf_op jit(solution)/shard_map/ppermute | solution.py:772
  34.5 8.3 %copy-start.22 = (bf16[384,768]{1,0:T(8,128)(2,1)}, bf16[384,768]{1,0:T(8,128)(2,1)S(1)}, u32[]{:S(2)}) copy-start(bf16[384,768]{1,0:T(8,128)(2,1)S(1)} %collective-permute-done.2.rest_2_) | copy-start | bytes 1769476
  37.5 5.2 %copy-start.11 = (bf16[512,768]{1,0:T(8,128)(2,1)}, bf16[512,768]{1,0:T(8,128)(2,1)S(1)}, u32[]{:S(2)}) copy-start(bf16[512,768]{1,0:T(8,128)(2,1)S(1)} %collective-permute-done.4.x_ref) | copy-start | bytes 2359300
  37.5 2.0 collective-permute-start.5
  39.5 19.6 %collective-permute-start.6 = (bf16[512,768]{1,0:T(8,128)(2,1)S(1)}, bf16[512,768]{1,0:T(8,128)(2,1)S(1)}, u32[]{:S(2)}, u32[]{:S(2)}) collective-permute-start(bf16[512,768]{1,0:T(8,128)(2,1)S(1)} %get-tuple-element.268), channel_id=1, source_target_pairs={{0,16},{16,0},{1,17},{17,1},{2,18},{18,2},{3,19},{19,3},{4,20},{20... | collective-permute-start | bytes 2359304 | tf_op jit(solution)/shard_map/ppermute | solution.py:772
  96.7 17.1 %copy-start.5 = (bf16[1536,768]{1,0:T(8,128)(2,1)S(1)}, bf16[1536,768]{1,0:T(8,128)(2,1)}, u32[]{:S(2)}) copy-start(bf16[1536,768]{1,0:T(8,128)(2,1)} %get-tuple-element.314) | copy-start | bytes 7077892
  96.7 17.0 %collective-permute-start.7 = (bf16[1536,768]{1,0:T(8,128)(2,1)}, bf16[1536,768]{1,0:T(8,128)(2,1)}, u32[]{:S(2)}, u32[]{:S(2)}) collective-permute-start(bf16[1536,768]{1,0:T(8,128)(2,1)} %get-tuple-element.309), channel_id=1, source_target_pairs={{0,1},{1,0},{2,3},{3,2},{4,5},{5,4},{6,7},{7,6},{8,9},{9,8},{10,11... | collective-permute-start | bytes 7077896 | tf_op jit(solution)/shard_map/ppermute | solution.py:772
  115.3 28.2 %collective-permute-start.8 = (bf16[1536,768]{1,0:T(8,128)(2,1)}, bf16[1536,768]{1,0:T(8,128)(2,1)}, u32[]{:S(2)}, u32[]{:S(2)}) collective-permute-start(bf16[1536,768]{1,0:T(8,128)(2,1)} %get-tuple-element.326), channel_id=1, source_target_pairs={{0,1},{1,0},{2,3},{3,2},{4,5},{5,4},{6,7},{7,6},{8,9},{9,8},{10,11... | collective-permute-start | bytes 7077896 | tf_op jit(solution)/shard_map/ppermute | solution.py:772
  115.7 27.8 %collective-permute-start.10 = (bf16[384,768]{1,0:T(8,128)(2,1)S(1)}, bf16[384,768]{1,0:T(8,128)(2,1)}, u32[]{:S(2)}, u32[]{:S(2)}) collective-permute-start(bf16[384,768]{1,0:T(8,128)(2,1)S(1)} %get-tuple-element.328), channel_id=1, source_target_pairs={{0,4},{1,5},{2,6},{3,7},{4,0},{5,1},{6,2},{7,3},{8,12},{9,13},{10,... | collective-permute-start | bytes 1769480 | tf_op jit(solution)/shard_map/ppermute | solution.py:772
  117.2 26.3 %collective-permute-start.9 = (bf16[384,768]{1,0:T(8,128)(2,1)S(1)}, bf16[384,768]{1,0:T(8,128)(2,1)}, u32[]{:S(2)}, u32[]{:S(2)}) collective-permute-start(bf16[384,768]{1,0:T(8,128)(2,1)S(1)} %get-tuple-element.327), channel_id=1, source_target_pairs={{0,2},{1,3},{2,0},{3,1},{4,6},{5,7},{6,4},{7,5},{8,10},{9,11},{10,... | collective-permute-start | bytes 1769480 | tf_op jit(solution)/shard_map/ppermute | solution.py:772
  148.3 20.5 %collective-permute-start.11 = (bf16[384,768]{1,0:T(8,128)(2,1)}, bf16[384,768]{1,0:T(8,128)(2,1)}, u32[]{:S(2)}, u32[]{:S(2)}) collective-permute-start(bf16[384,768]{1,0:T(8,128)(2,1)} %get-tuple-element.348), channel_id=1, source_target_pairs={{0,1},{1,0},{2,3},{3,2},{4,5},{5,4},{6,7},{7,6},{8,9},{9,8},{10,11... | collective-permute-start | bytes 1769480 | tf_op jit(solution)/shard_map/ppermute | solution.py:772
  148.3 20.5 %collective-permute-start.12 = (bf16[192,768]{1,0:T(8,128)(2,1)}, bf16[192,768]{1,0:T(8,128)(2,1)}, u32[]{:S(2)}, u32[]{:S(2)}) collective-permute-start(bf16[192,768]{1,0:T(8,128)(2,1)} %add_convert_fusion.12), channel_id=1, source_target_pairs={{0,8},{1,9},{2,10},{3,11},{4,12},{5,13},{6,14},{7,15},{8,0},{9,1},... | collective-permute-start | bytes 884744 | tf_op jit(solution)/shard_map/ppermute | solution.py:772
  150.9 31.5 %collective-permute-start.14 = (bf16[768,768]{1,0:T(8,128)(2,1)}, bf16[768,768]{1,0:T(8,128)(2,1)}, u32[]{:S(2)}, u32[]{:S(2)}) collective-permute-start(bf16[768,768]{1,0:T(8,128)(2,1)} %add_convert_fusion.1), channel_id=1, source_target_pairs={{0,2},{1,3},{2,0},{3,1},{4,6},{5,7},{6,4},{7,5},{8,10},{9,11},{10,... | collective-permute-start | bytes 3538952 | tf_op jit(solution)/shard_map/ppermute | solution.py:772
  172.5 9.9 %collective-permute-start.13 = (bf16[192,768]{1,0:T(8,128)(2,1)S(1)}, bf16[192,768]{1,0:T(8,128)(2,1)S(1)}, u32[]{:S(2)}, u32[]{:S(2)}) collective-permute-start(bf16[192,768]{1,0:T(8,128)(2,1)S(1)} %broadcast_select_fusion.2), channel_id=1, source_target_pairs={{0,4},{1,5},{2,6},{3,7},{4,0},{5,1},{6,2},{7,3},{8,12},{9,13},{10,... | collective-permute-start | bytes 884744 | tf_op jit(solution)/shard_map/ppermute | solution.py:772
  172.9 9.5 %copy-start.6 = (bf16[1536,768]{1,0:T(8,128)(2,1)S(1)}, bf16[1536,768]{1,0:T(8,128)(2,1)}, u32[]{:S(2)}) copy-start(bf16[1536,768]{1,0:T(8,128)(2,1)} %get-tuple-element.341) | copy-start | bytes 7077892
  172.9 24.0 %collective-permute-start.17 = (bf16[288,768]{1,0:T(8,128)(2,1)}, bf16[288,768]{1,0:T(8,128)(2,1)}, u32[]{:S(2)}, u32[]{:S(2)}) collective-permute-start(bf16[288,768]{1,0:T(8,128)(2,1)} %pad_maximum_fusion.2), channel_id=1, source_target_pairs={{0,2},{1,3},{2,0},{3,1},{4,6},{5,7},{6,4},{7,5},{8,10},{9,11},{10,... | collective-permute-start | bytes 1327112 | tf_op jit(solution)/shard_map/ppermute | solution.py:772
  186.3 10.6 %collective-permute-start.15 = (bf16[768,768]{1,0:T(8,128)(2,1)}, bf16[768,768]{1,0:T(8,128)(2,1)}, u32[]{:S(2)}, u32[]{:S(2)}) collective-permute-start(bf16[768,768]{1,0:T(8,128)(2,1)} %get-tuple-element.374), channel_id=1, source_target_pairs={{0,1},{1,0},{2,3},{3,2},{4,5},{5,4},{6,7},{7,6},{8,9},{9,8},{10,11... | collective-permute-start | bytes 3538952 | tf_op jit(solution)/shard_map/ppermute | solution.py:772
  186.3 10.6 %collective-permute-start.16 = (bf16[192,768]{1,0:T(8,128)(2,1)}, bf16[192,768]{1,0:T(8,128)(2,1)}, u32[]{:S(2)}, u32[]{:S(2)}) collective-permute-start(bf16[192,768]{1,0:T(8,128)(2,1)} %broadcast_select_fusion.1), channel_id=1, source_target_pairs={{0,4},{1,5},{2,6},{3,7},{4,0},{5,1},{6,2},{7,3},{8,12},{9,13},{10,... | collective-permute-start | bytes 884744 | tf_op jit(solution)/shard_map/ppermute | solution.py:772
  187.9 8.9 %copy-start.2 = (bf16[768,768]{1,0:T(8,128)(2,1)S(1)}, bf16[768,768]{1,0:T(8,128)(2,1)}, u32[]{:S(2)}) copy-start(bf16[768,768]{1,0:T(8,128)(2,1)} %copy-done.1) | copy-start | bytes 3538948
  187.9 9.0 %copy-start.20 = (bf16[384,768]{1,0:T(8,128)(2,1)S(1)}, bf16[384,768]{1,0:T(8,128)(2,1)}, u32[]{:S(2)}) copy-start(bf16[384,768]{1,0:T(8,128)(2,1)} %get-tuple-element.355) | copy-start | bytes 1769476
  201.5 15.9 %copy-start.8 = (f32[192,768]{1,0:T(8,128)S(1)}, f32[192,768]{1,0:T(8,128)}, u32[]{:S(2)}) copy-start(f32[192,768]{1,0:T(8,128)} %copy-done.7) | copy-start | bytes 1769476
  201.5 15.6 %collective-permute-start.18 = (bf16[384,768]{1,0:T(8,128)(2,1)S(1)}, bf16[384,768]{1,0:T(8,128)(2,1)}, u32[]{:S(2)}, u32[]{:S(2)}) collective-permute-start(bf16[384,768]{1,0:T(8,128)(2,1)S(1)} %add_convert_fusion.2), channel_id=1, source_target_pairs={{0,2},{1,3},{2,0},{3,1},{4,6},{5,7},{6,4},{7,5},{8,10},{9,11},{10,... | collective-permute-start | bytes 1769480 | tf_op jit(solution)/shard_map/ppermute | solution.py:772
  202.2 13.7 %collective-permute-start.19 = (bf16[288,768]{1,0:T(8,128)(2,1)S(1)}, bf16[288,768]{1,0:T(8,128)(2,1)}, u32[]{:S(2)}, u32[]{:S(2)}) collective-permute-start(bf16[288,768]{1,0:T(8,128)(2,1)S(1)} %bitcast.98), channel_id=1, source_target_pairs={{0,4},{1,5},{2,6},{3,7},{4,0},{5,1},{6,2},{7,3},{8,12},{9,13},{10,... | collective-permute-start | bytes 1327112 | tf_op jit(solution)/shard_map/ppermute | solution.py:772
  215.9 4.6 %copy-start.12 = (bf16[512,768]{1,0:T(8,128)(2,1)S(1)}, bf16[512,768]{1,0:T(8,128)(2,1)}, u32[]{:S(2)}) copy-start(bf16[512,768]{1,0:T(8,128)(2,1)} %get-tuple-element.400) | copy-start | bytes 2359300
  217.1 3.5 %collective-permute-start.20 = (bf16[512,768]{1,0:T(8,128)(2,1)}, bf16[512,768]{1,0:T(8,128)(2,1)}, u32[]{:S(2)}, u32[]{:S(2)}) collective-permute-start(bf16[512,768]{1,0:T(8,128)(2,1)} %get-tuple-element.403), channel_id=1, source_target_pairs={{0,1},{1,0},{2,3},{3,2},{4,5},{5,4},{6,7},{7,6},{8,9},{9,8},{10,11... | collective-permute-start | bytes 2359304 | tf_op jit(solution)/shard_map/ppermute | solution.py:772
  217.1 31.0 %collective-permute-start.26 = (bf16[192,768]{1,0:T(8,128)(2,1)}, bf16[192,768]{1,0:T(8,128)(2,1)}, u32[]{:S(2)}, u32[]{:S(2)}) collective-permute-start(bf16[192,768]{1,0:T(8,128)(2,1)} %get-tuple-element.416), channel_id=1, source_target_pairs={{0,8},{1,9},{2,10},{3,11},{4,12},{5,13},{6,14},{7,15},{8,0},{9,1},... | collective-permute-start | bytes 884744 | tf_op jit(solution)/shard_map/ppermute | solution.py:772
  219.0 42.8 %collective-permute-start.31 = (bf16[1024,768]{1,0:T(8,128)(2,1)}, bf16[1024,768]{1,0:T(8,128)(2,1)}, u32[]{:S(2)}, u32[]{:S(2)}) collective-permute-start(bf16[1024,768]{1,0:T(8,128)(2,1)} %get-tuple-element.423), channel_id=1, source_target_pairs={{0,16},{16,0},{1,17},{17,1},{2,18},{18,2},{3,19},{19,3},{4,20},{20... | collective-permute-start | bytes 4718600 | tf_op jit(solution)/shard_map/ppermute | solution.py:772
  226.5 18.2 %copy-start.13 = (bf16[512,768]{1,0:T(8,128)(2,1)S(1)}, bf16[512,768]{1,0:T(8,128)(2,1)}, u32[]{:S(2)}) copy-start(bf16[512,768]{1,0:T(8,128)(2,1)} %get-tuple-element.400) | copy-start | bytes 2359300
  226.5 18.2 %collective-permute-start.21 = (bf16[256,768]{1,0:T(8,128)(2,1)}, bf16[256,768]{1,0:T(8,128)(2,1)}, u32[]{:S(2)}, u32[]{:S(2)}) collective-permute-start(bf16[256,768]{1,0:T(8,128)(2,1)} %add_convert_fusion.6), channel_id=1, source_target_pairs={{0,2},{1,3},{2,0},{3,1},{4,6},{5,7},{6,4},{7,5},{8,10},{9,11},{10,... | collective-permute-start | bytes 1179656 | tf_op jit(solution)/shard_map/ppermute | solution.py:772
  229.8 14.9 %collective-permute-start.22 = (bf16[192,768]{1,0:T(8,128)(2,1)}, bf16[192,768]{1,0:T(8,128)(2,1)S(1)}, u32[]{:S(2)}, u32[]{:S(2)}) collective-permute-start(bf16[192,768]{1,0:T(8,128)(2,1)} %add_convert_fusion.7), channel_id=1, source_target_pairs={{0,4},{1,5},{2,6},{3,7},{4,0},{5,1},{6,2},{7,3},{8,12},{9,13},{10,... | collective-permute-start | bytes 884744 | tf_op jit(solution)/shard_map/ppermute | solution.py:772
  231.0 1.2 collective-permute-start.23
  232.1 25.9 %collective-permute-start.29 = (bf16[144,768]{1,0:T(8,128)(2,1)S(1)}, bf16[144,768]{1,0:T(8,128)(2,1)S(1)}, u32[]{:S(2)}, u32[]{:S(2)}) collective-permute-start(bf16[144,768]{1,0:T(8,128)(2,1)S(1)} %fusion.8), channel_id=1, source_target_pairs={{0,8},{1,9},{2,10},{3,11},{4,12},{5,13},{6,14},{7,15},{8,0},{9,1},... | collective-permute-start | bytes 663560 | tf_op jit(solution)/shard_map/ppermute | solution.py:772
  245.8 8.2 %collective-permute-start.24 = (bf16[128,768]{1,0:T(8,128)(2,1)S(1)}, bf16[128,768]{1,0:T(8,128)(2,1)S(1)}, u32[]{:S(2)}, u32[]{:S(2)}) collective-permute-start(bf16[128,768]{1,0:T(8,128)(2,1)S(1)} %add_convert_fusion.13), channel_id=1, source_target_pairs={{0,4},{1,5},{2,6},{3,7},{4,0},{5,1},{6,2},{7,3},{8,12},{9,13},{10,... | collective-permute-start | bytes 589832 | tf_op jit(solution)/shard_map/ppermute | solution.py:772
  245.9 3.7 %collective-permute-start.25 = (f32[1,768]{1,0:T(1,128)S(1)}, f32[1,768]{1,0:T(1,128)S(1)}, u32[]{:S(2)}, u32[]{:S(2)}) collective-permute-start(f32[1,768]{1,0:T(1,128)S(1)} %add.260), channel_id=1, source_target_pairs={{0,2},{1,3},{2,0},{3,1},{4,6},{5,7},{6,4},{7,5},{8,10},{9,11},{10,... | collective-permute-start | bytes 9224 | tf_op jit(solution)/shard_map/ppermute | solution.py:772
  248.1 12.3 %collective-permute-start.30 = (bf16[96,768]{1,0:T(8,128)(2,1)S(1)}, bf16[96,768]{1,0:T(8,128)(2,1)S(1)}, u32[]{:S(2)}, u32[]{:S(2)}) collective-permute-start(bf16[96,768]{1,0:T(8,128)(2,1)S(1)} %add_convert_fusion.14), channel_id=1, source_target_pairs={{0,8},{1,9},{2,10},{3,11},{4,12},{5,13},{6,14},{7,15},{8,0},{9,1},... | collective-permute-start | bytes 442376 | tf_op jit(solution)/shard_map/ppermute | solution.py:772
  255.0 6.8 %collective-permute-start.27 = (bf16[64,768]{1,0:T(8,128)(2,1)S(1)}, bf16[64,768]{1,0:T(8,128)(2,1)S(1)}, u32[]{:S(2)}, u32[]{:S(2)}) collective-permute-start(bf16[64,768]{1,0:T(8,128)(2,1)S(1)} %add_convert_fusion.15), channel_id=1, source_target_pairs={{0,8},{1,9},{2,10},{3,11},{4,12},{5,13},{6,14},{7,15},{8,0},{9,1},... | collective-permute-start | bytes 294920 | tf_op jit(solution)/shard_map/ppermute | solution.py:772
  255.1 5.2 %collective-permute-start.28 = (f32[1,768]{1,0:T(1,128)S(1)}, f32[1,768]{1,0:T(1,128)S(1)}, u32[]{:S(2)}, u32[]{:S(2)}) collective-permute-start(f32[1,768]{1,0:T(1,128)S(1)} %add.265), channel_id=1, source_target_pairs={{0,4},{1,5},{2,6},{3,7},{4,0},{5,1},{6,2},{7,3},{8,12},{9,13},{10,... | collective-permute-start | bytes 9224 | tf_op jit(solution)/shard_map/ppermute | solution.py:772
  263.9 4.7 %copy-start.14 = (f32[48,768]{1,0:T(8,128)S(1)}, f32[48,768]{1,0:T(8,128)}, u32[]{:S(2)}) copy-start(f32[48,768]{1,0:T(8,128)} %get-tuple-element.468) | copy-start | bytes 442372
  265.7 12.7 %collective-permute-start.33 = (f32[64,768]{1,0:T(8,128)S(1)}, f32[64,768]{1,0:T(8,128)S(1)}, u32[]{:S(2)}, u32[]{:S(2)}) collective-permute-start(f32[64,768]{1,0:T(8,128)S(1)} %convert_add_fusion.5), channel_id=1, source_target_pairs={{0,16},{16,0},{1,17},{17,1},{2,18},{18,2},{3,19},{19,3},{4,20},{20... | collective-permute-start | bytes 589832 | tf_op jit(solution)/shard_map/ppermute | solution.py:772
  267.5 10.9 %collective-permute-start.32 = (bf16[96,768]{1,0:T(8,128)(2,1)S(1)}, bf16[96,768]{1,0:T(8,128)(2,1)S(1)}, u32[]{:S(2)}, u32[]{:S(2)}) collective-permute-start(bf16[96,768]{1,0:T(8,128)(2,1)S(1)} %get-tuple-element.435), channel_id=1, source_target_pairs={{0,16},{16,0},{1,17},{17,1},{2,18},{18,2},{3,19},{19,3},{4,20},{20... | collective-permute-start | bytes 442376 | tf_op jit(solution)/shard_map/ppermute | solution.py:772
  267.8 10.6 %collective-permute-start.34 = (f32[1,768]{1,0:T(1,128)S(1)}, f32[1,768]{1,0:T(1,128)S(1)}, u32[]{:S(2)}, u32[]{:S(2)}) collective-permute-start(f32[1,768]{1,0:T(1,128)S(1)} %add.278), channel_id=1, source_target_pairs={{0,8},{1,9},{2,10},{3,11},{4,12},{5,13},{6,14},{7,15},{8,0},{9,1},... | collective-permute-start | bytes 9224 | tf_op jit(solution)/shard_map/ppermute | solution.py:772
  (21 other events, 51.1 us)

commit v2 on v1

--- a/solution.py
+++ b/solution.py
@@ -710,7 +710,7 @@
     count = len(grads) // 3
     last = count > 1
     part = grads[-1].shape[1]
-    tile = 256 if last else 512
+    tile = 256
     rows = pl.BlockSpec((tile, width), lambda i, *_: (i, 0))
     extra = last and relative
     kept, sent = block_shapes(width * part // UNIT + (256 if extra else 0), width, relative)

time: 286 us -> 286 us (level)
  no operation moved by 1% of the time
where the time goes in v2:
time: 286 us; the launch traced here: 282 us
  Pallas kernels  155 us (54%)
  other arithmetic  46.2 us (16%)
  waiting for transfers between devices  37.6 us (13%)
  starting transfers between devices  28.6 us (10%)
  local copies, waits for them, and re-layouts  8.6 us (3%)
  matrix products  4.07 us (1%)
    pallas_call x2, Pallas kernels, feed_call(): pl.pallas_call(functools.partial(feed_kernel, first=first, blocks=blocks,...  39.4 us
    ppermute x35, waiting for transfers between devices, swapped(): return lax.ppermute(value, axis, pairs)  37.6 us
    ppermute x35, starting transfers between devices, swapped(): return lax.ppermute(value, axis, pairs)  28.6 us
    pallas_call x2, Pallas kernels, attend_back_call(): pl.pallas_call(attend_back_kernel, grid=(pages, pairs // PAIRS), in_specs...  24.7 us
    pallas_call x1, Pallas kernels, finish_call(): pl.pallas_call(functools.partial(finish_kernel, blocks=blocks, tile=tile,...  24.1 us
    pallas_call x2, Pallas kernels, weights_call(): pl.pallas_call(functools.partial(weights_kernel, start=start, count=count...  21 us
    pallas_call x2, Pallas kernels, attend_call(): pl.pallas_call(attend_kernel, grid=(1, width // 128 // PAIRS), in_specs=[...  17.1 us
    pallas_call x2, Pallas kernels, pair_call(): pl.pallas_call(functools.partial(pair_kernel, count=len(pieces)), grid_sp...  11.2 us
  transfers between devices with their start and end apart: 35, of which 12 were waited for; matrix products, arithmetic and copies ran while one was open for 13% of the time, Pallas kernels for 42%

profile of v2, /device:TPU:0, one launch (start us, length us, event | category | flops | bytes accessed | tf_op | source)
XLA Modules:
  0.0 281.5 jit_solution(986379530683258865)
XLA Ops:
  0.7 1.4 select_bitcast_fusion
  2.1 3.0 %collective-permute-start = (bf16[384,768]{1,0:T(8,128)(2,1)S(1)}, bf16[384,768]{1,0:T(8,128)(2,1)S(1)}, u32[]{:S(2)}, u32[]{:S(2)}) collective-permute-start(bf16[384,768]{1,0:T(8,128)(2,1)S(1)} %select_bitcast_fusion), channel_id=1, source_target_pairs={{0,16},{16,0},{1,17},{17,1},{2,18},{18,2},{3,19},{19,3},{4,20},{20... | collective-permute-start | bytes 1769480 | tf_op jit(solution)/shard_map/ppermute | solution.py:772
  12.0 5.7 %query.1 = (bf16[1024,768]{1,0:T(8,128)(2,1)}, bf16[1024,768]{1,0:T(8,128)(2,1)}) custom-call(bf16[1024,768]{1,0:T(8,128)(2,1)} %bitcast.76, f32[1,768]{1,0:T(1,128)} %gain_ref.3, f32[1,768]{1,0:T(1,128)} %shift_ref, bf16[768,768]{1,0:T(8,128)(2,1)} %bitcast.90, f32[1,768]{1,0:T(1,128)} %b_ref), custom_call_target="tpu_custom_call" | custom-call | flops 18874368 | bytes 92160 | tf_op jit(solution)/shard_map/query/pallas_call | solution.py:71
  18.8 1.8 collective-permute-start.4
  20.6 1.5 collective-permute-start.2
  22.0 5.2 %picks.1.picks_ref = bf16[1024,1536]{1,0:T(8,128)(2,1)} custom-call(bf16[2,512,64]{2,1,0:T(8,128)(2,1)} %fusion.5.hq_ref, bf16[2,12,64,128]{3,2,1,0:T(8,128)(2,1)} %pad_maximum_fusion.3.bias_ref), custom_call_target="tpu_custom_call" | custom-call | flops 3145728 | bytes 49152 | tf_op jit(solution)/shard_map/picks/pallas_call | solution.py:158
  27.2 7.2 %collective-permute-done.2.rest_2_ = bf16[384,768]{1,0:T(8,128)(2,1)S(1)} collective-permute-done((bf16[384,768]{1,0:T(8,128)(2,1)S(1)}, bf16[384,768]{1,0:T(8,128)(2,1)S(1)}, u32[]{:S(2)}, u32[]{:S(2)}) %collective-permute-start.2) | collective-permute-done | bytes 589856 | tf_op jit(solution)/shard_map/ppermute | solution.py:772
  34.5 3.1 %collective-permute-done.4.x_ref = bf16[512,768]{1,0:T(8,128)(2,1)S(1)} collective-permute-done((bf16[512,768]{1,0:T(8,128)(2,1)S(1)}, bf16[512,768]{1,0:T(8,128)(2,1)S(1)}, u32[]{:S(2)}, u32[]{:S(2)}) %collective-permute-start.4) | collective-permute-done | bytes 786464 | tf_op jit(solution)/shard_map/ppermute | solution.py:772
  37.5 2.0 collective-permute-done.5.rest_3_
  39.5 1.4 collective-permute-start.6
  42.7 6.0 %pair.2 = (bf16[1024,768]{1,0:T(8,128)(2,1)}, bf16[1024,768]{1,0:T(8,128)(2,1)}, bf16[1024,768]{1,0:T(8,128)(2,1)}, bf16[1024,768]{1,0:T(8,128)(2,1)}, bf16[4,384,768]{2,1,0:T(8,128)(2,1)}) custom-call(s32[1]{0:T(128)} %bitcast.me_ref, bf16[512,768]{1,0:T(8,128)(2,1)} %copy-done.11, f32[3,768]{1,0:T(4,128)} %copy-done.26, bf16[384,768]{1,0:T(8,128)(2,1)} %copy-done.21, ...), custom_call_target="tpu_custom_call" | custom-call | flops 18874368 | bytes 49152 | tf_op jit(solution)/shard_map/pair/pallas_call | solution.py:133
  48.7 8.6 %attend.2 = (bf16[1024,768]{1,0:T(8,128)(2,1)}, f32[2,6,2,512]{3,2,1,0:T(2,128)}) custom-call(bf16[1024,768]{1,0:T(8,128)(2,1)} %get-tuple-element.263.q_ref, bf16[1024,768]{1,0:T(8,128)(2,1)} %get-tuple-element.280.k_ref.rest_2_, bf16[1024,768]{1,0:T(8,128)(2,1)} %get-tuple-element.281.v_ref.rest_3_, bf16[1024,1536]{1,0:T(8,128)(2,1)} %picks.1.picks_ref, ...), custom_call_target="tpu_custom_call" | custom-call | flops 50331648 | bytes 49152 | tf_op jit(solution)/shard_map/attend/pallas_call | solution.py:223
  57.3 1.9 collective-permute-done.6.x_ref
  60.0 5.2 %pair.3 = (bf16[1024,768]{1,0:T(8,128)(2,1)}, bf16[1024,768]{1,0:T(8,128)(2,1)}, bf16[1024,768]{1,0:T(8,128)(2,1)}, bf16[1024,768]{1,0:T(8,128)(2,1)}) custom-call(s32[1]{0:T(128)} %bitcast.me_ref, bf16[512,768]{1,0:T(8,128)(2,1)} %copy-done.10, f32[3,768]{1,0:T(4,128)} %copy-done.26, ...), custom_call_target="tpu_custom_call", output_to_operand_aliasing={{0}: (4, {}), {1}: (5, {}), {2}: (6, {}), {3}: (7, {})} | custom-call | flops 18874368 | bytes 49152 | tf_op jit(solution)/shard_map/pair/pallas_call | solution.py:133
  65.2 8.5 %attend.3 = (bf16[1024,768]{1,0:T(8,128)(2,1)}, f32[2,6,2,512]{3,2,1,0:T(2,128)}) custom-call(bf16[1024,768]{1,0:T(8,128)(2,1)} %get-tuple-element.263.q_ref, bf16[1024,768]{1,0:T(8,128)(2,1)} %get-tuple-element.334.k_ref, bf16[1024,768]{1,0:T(8,128)(2,1)} %get-tuple-element.335.v_ref, ...), custom_call_target="tpu_custom_call", output_to_operand_aliasing={{0}: (5, {}), {1}: (6, {})} | custom-call | flops 50331648 | bytes 49152 | tf_op jit(solution)/shard_map/attend/pallas_call | solution.py:223
  74.3 22.4 %feed.2 = (f32[1024,768]{1,0:T(8,128)}, bf16[1024,768]{1,0:T(8,128)(2,1)}, bf16[1024,3072]{1,0:T(8,128)(2,1)}, bf16[1024,3072]{1,0:T(8,128)(2,1)}, f32[24,768]{1...) custom-call(s32[1]{0:T(128)} %bitcast.me_ref, bf16[1024,768]{1,0:T(8,128)(2,1)} %bitcast.77, ...), custom_call_target="tpu_custom_call" | custom-call | flops 150994944 | bytes 245760 | tf_op jit(solution)/shard_map/feed/pallas_call | solution.py:459
  96.8 17.0 %feed.3 = (bf16[1024,3072]{1,0:T(8,128)(2,1)}, bf16[1024,3072]{1,0:T(8,128)(2,1)}, f32[24,768]{1,0:T(8,128)}, bf16[1536,768]{1,0:T(8,128)(2,1)}, bf16[1536,768]{1,0:T(8,128)(2,1)}) custom-call(s32[1]{0:T(128)} %bitcast.me_ref, bf16[1024,768]{1,0:T(8,128)(2,1)} %get-tuple-element.300.rest_0_, ...), custom_call_target="tpu_custom_call", output_to_operand_aliasing={{0}: (7, {}), {1}: (8, {})} | custom-call | flops 150994944 | bytes 245760 | tf_op jit(solution)/shard_map/feed/pallas_call | solution.py:459
  113.8 1.5 add_convert_fusion.4
  115.7 1.5 collective-permute-start.10
  117.2 1.5 collective-permute-start.9
  119.4 24.1 %finish.1 = (bf16[1024,768]{1,0:T(8,128)(2,1)}, f32[1024,768]{1,0:T(8,128)}, bf16[1024,768]{1,0:T(8,128)(2,1)}, f32[24,768]{1,0:T(8,128)}, bf16[384,768]{1,0:T(8,128)(2,1)}, /*index=5*/bf16[384,768]{1,0:T(8,128)(2,1)}) custom-call(s32[1]{0:T(128)} %bitcast.me_ref, bf16[1024,3072]{1,0:T(8,128)(2,1)} %get-tuple-element.316.act_ref, ...), custom_call_target="tpu_custom_call" | custom-call | flops 37748736 | bytes 294912 | tf_op jit(solution)/shard_map/finish/pallas_call | solution.py:608
  143.5 1.9 add_convert_fusion.12
  145.4 2.9 %add_convert_fusion.1 = bf16[768,768]{1,0:T(8,128)(2,1)} fusion(bf16[1536,768]{1,0:T(8,128)(2,1)} %collective-permute-done.8, bf16[1536,768]{1,0:T(8,128)(2,1)} %get-tuple-element.341), kind=kLoop, calls=%fused_computation.1 | loop fusion | flops 2359296 | bytes 3538944 | tf_op jit(solution)/shard_map/convert_element_type | solution.py:776
  148.3 2.6 collective-permute-start.12
  151.4 15.8 %attend_back.2 = (bf16[1024,512]{1,0:T(8,128)(2,1)}, bf16[1024,512]{1,0:T(8,128)(2,1)}, bf16[1024,512]{1,0:T(8,128)(2,1)}, f32[2,8,64,64]{3,2,1,0:T(8,128)}) custom-call(bf16[1024,768]{1,0:T(8,128)(2,1)} %get-tuple-element.263.q_ref, bf16[1024,768]{1,0:T(8,128)(2,1)} %get-tuple-element.334.k_ref, bf16[1024,768]{1,0:T(8,128)(2,1)} %get-tuple-element.335.v_ref, ...), custom_call_target="tpu_custom_call" | custom-call | flops 687194767360 | bytes 536870912 | tf_op jit(solution)/shard_map/attend_back/pallas_call | solution.py:305
  167.3 1.6 add_convert_fusion.3
  169.0 1.6 convert_add_fusion.1
  173.1 1.5 collective-permute-start.17
  174.6 8.0 %weights.2 = (f32[24,768]{1,0:T(8,128)}, bf16[768,768]{1,0:T(8,128)(2,1)}, bf16[768,768]{1,0:T(8,128)(2,1)}) custom-call(s32[1]{0:T(128)} %bitcast.me_ref, bf16[1024,768]{1,0:T(8,128)(2,1)} %get-tuple-element.331.n_ref, bf16[1024,768]{1,0:T(8,128)(2,1)} %get-tuple-element.332.np_ref, bf16[1024,512]{1,0:T(8,128)(2,1)} %get-tuple-element.385.rest_0_, ...), custom_call_target="tpu_custom_call" | custom-call | flops 37748736 | bytes 294912 | tf_op jit(solution)/shard_map/weights/pallas_call | solution.py:734
  182.7 2.1 add_convert_fusion
  186.6 1.6 collective-permute-start.16
  188.2 8.9 %attend_back.3 = (bf16[1024,256]{1,0:T(8,128)(2,1)}, bf16[1024,256]{1,0:T(8,128)(2,1)}, bf16[1024,256]{1,0:T(8,128)(2,1)}, f32[2,4,64,64]{3,2,1,0:T(8,128)}) custom-call(bf16[1024,768]{1,0:T(8,128)(2,1)} %get-tuple-element.263.q_ref, bf16[1024,768]{1,0:T(8,128)(2,1)} %get-tuple-element.334.k_ref, bf16[1024,768]{1,0:T(8,128)(2,1)} %get-tuple-element.335.v_ref, ...), custom_call_target="tpu_custom_call" | custom-call | flops 343597383680 | bytes 268435456 | tf_op jit(solution)/shard_map/attend_back/pallas_call | solution.py:305
  199.8 1.9 broadcast_select_fusion
  203.1 13.0 %weights.3 = (f32[1024,768]{1,0:T(8,128)}, bf16[1024,768]{1,0:T(8,128)(2,1)}, f32[24,768]{1,0:T(8,128)}, bf16[512,768]{1,0:T(8,128)(2,1)}, bf16[512,768]{1,0:T(8,128)(2,1)}) custom-call(s32[1]{0:T(128)} %bitcast.me_ref, bf16[1024,768]{1,0:T(8,128)(2,1)} %get-tuple-element.331.n_ref, bf16[1024,768]{1,0:T(8,128)(2,1)} %get-tuple-element.332.np_ref, ...), custom_call_target="tpu_custom_call" | custom-call | flops 18874368 | bytes 294912 | tf_op jit(solution)/shard_map/weights/pallas_call | solution.py:734
  219.3 1.5 collective-permute-start.31
  220.8 1.8 add_convert_fusion.6
  224.8 2.0 add_convert_fusion.7
  228.8 1.3 convolution_bitcast_fusion
  232.3 2.6 collective-permute-start.29
  234.9 10.2 %collective-permute-done.22 = bf16[192,768]{1,0:T(8,128)(2,1)S(1)} collective-permute-done((bf16[192,768]{1,0:T(8,128)(2,1)}, bf16[192,768]{1,0:T(8,128)(2,1)S(1)}, u32[]{:S(2)}, u32[]{:S(2)}) %collective-permute-start.22) | collective-permute-done | bytes 294944 | tf_op jit(solution)/shard_map/ppermute | solution.py:772
  248.4 1.6 collective-permute-done.25
  250.0 4.4 %collective-permute-done.24 = bf16[128,768]{1,0:T(8,128)(2,1)S(1)} collective-permute-done((bf16[128,768]{1,0:T(8,128)(2,1)S(1)}, bf16[128,768]{1,0:T(8,128)(2,1)S(1)}, u32[]{:S(2)}, u32[]{:S(2)}) %collective-permute-start.24) | collective-permute-done | bytes 196640 | tf_op jit(solution)/shard_map/ppermute | solution.py:772
  255.6 1.9 convert_add_fusion
  257.4 3.0 %collective-permute-done.30 = bf16[96,768]{1,0:T(8,128)(2,1)S(1)} collective-permute-done((bf16[96,768]{1,0:T(8,128)(2,1)S(1)}, bf16[96,768]{1,0:T(8,128)(2,1)S(1)}, u32[]{:S(2)}, u32[]{:S(2)}) %collective-permute-start.30) | collective-permute-done | bytes 147488 | tf_op jit(solution)/shard_map/ppermute | solution.py:772
  260.5 1.6 collective-permute-done.27
  266.0 1.8 collective-permute-start.33
  270.2 1.3 fusion.20
  271.5 6.6 %tokens.1 = f32[1024,768]{1,0:T(8,128)} custom-call(bf16[1024,768]{1,0:T(8,128)(2,1)} %bitcast.79, f32[1,768]{1,0:T(1,128)} %gain_ref.3, f32[1024,768]{1,0:T(8,128)} %get-tuple-element.430.gm_ref, f32[1024,768]{1,0:T(8,128)} %get-tuple-element.431.gq_ref, bf16[1024,768]{1,0:T(8,128)(2,1)} %collective-permute-done.31.gf_ref), custom_call_target="tpu_custom_call" | custom-call | flops 245760 | bytes 196608 | tf_op jit(solution)/shard_map/tokens/pallas_call | solution.py:758
  (188 shorter events, 44.4 us)
Async XLA Ops:
  0.7 4.7 %copy-start.32 = (f32[1,768]{1,0:T(1,128)S(1)}, f32[1,768]{1,0:T(1,128)}, u32[]{:S(2)}) copy-start(f32[1,768]{1,0:T(1,128)} %param.37) | copy-start | bytes 9220
  2.1 16.6 %collective-permute-start = (bf16[384,768]{1,0:T(8,128)(2,1)S(1)}, bf16[384,768]{1,0:T(8,128)(2,1)S(1)}, u32[]{:S(2)}, u32[]{:S(2)}) collective-permute-start(bf16[384,768]{1,0:T(8,128)(2,1)S(1)} %select_bitcast_fusion), channel_id=1, source_target_pairs={{0,16},{16,0},{1,17},{17,1},{2,18},{18,2},{3,19},{19,3},{4,20},{20... | collective-permute-start | bytes 1769480 | tf_op jit(solution)/shard_map/ppermute | solution.py:772
  5.2 13.6 %collective-permute-start.1 = (f32[3,768]{1,0:T(4,128)S(1)}, f32[3,768]{1,0:T(4,128)S(1)}, u32[]{:S(2)}, u32[]{:S(2)}) collective-permute-start(f32[3,768]{1,0:T(4,128)S(1)} %pad_maximum_fusion.8), channel_id=1, source_target_pairs={{0,16},{16,0},{1,17},{17,1},{2,18},{18,2},{3,19},{19,3},{4,20},{20... | collective-permute-start | bytes 27656 | tf_op jit(solution)/shard_map/ppermute | solution.py:772
  18.7 8.5 %copy-start.26 = (f32[3,768]{1,0:T(4,128)}, f32[3,768]{1,0:T(4,128)S(1)}, u32[]{:S(2)}) copy-start(f32[3,768]{1,0:T(4,128)S(1)} %collective-permute-done.1.rows_ref) | copy-start | bytes 27652
  18.7 8.5 %copy-start.21 = (bf16[384,768]{1,0:T(8,128)(2,1)}, bf16[384,768]{1,0:T(8,128)(2,1)S(1)}, u32[]{:S(2)}) copy-start(bf16[384,768]{1,0:T(8,128)(2,1)S(1)} %collective-permute-done.rest_0_) | copy-start | bytes 1769476
  18.8 18.8 %collective-permute-start.4 = (bf16[512,768]{1,0:T(8,128)(2,1)S(1)}, bf16[512,768]{1,0:T(8,128)(2,1)S(1)}, u32[]{:S(2)}, u32[]{:S(2)}) collective-permute-start(bf16[512,768]{1,0:T(8,128)(2,1)S(1)} %get-tuple-element.248), channel_id=1, source_target_pairs={{0,16},{16,0},{1,17},{17,1},{2,18},{18,2},{3,19},{19,3},{4,20},{20... | collective-permute-start | bytes 2359304 | tf_op jit(solution)/shard_map/ppermute | solution.py:772
  20.6 13.9 %collective-permute-start.2 = (bf16[384,768]{1,0:T(8,128)(2,1)S(1)}, bf16[384,768]{1,0:T(8,128)(2,1)S(1)}, u32[]{:S(2)}, u32[]{:S(2)}) collective-permute-start(bf16[384,768]{1,0:T(8,128)(2,1)S(1)} %collective-permute-done.rest_0_), channel_id=1, source_target_pairs={{0,2},{1,3},{2,0},{3,1},{4,6},{5,7},{6,4},{7,5},{8,10},{9,11},{10,... | collective-permute-start | bytes 1769480 | tf_op jit(solution)/shard_map/ppermute | solution.py:772
  22.0 12.4 %collective-permute-start.3 = (bf16[384,768]{1,0:T(8,128)(2,1)S(1)}, bf16[384,768]{1,0:T(8,128)(2,1)}, u32[]{:S(2)}, u32[]{:S(2)}) collective-permute-start(bf16[384,768]{1,0:T(8,128)(2,1)S(1)} %collective-permute-done.rest_0_), channel_id=1, source_target_pairs={{0,1},{1,0},{2,3},{3,2},{4,5},{5,4},{6,7},{7,6},{8,9},{9,8},{10,11... | collective-permute-start | bytes 1769480 | tf_op jit(solution)/shard_map/ppermute | solution.py:772
  34.5 8.3 %copy-start.22 = (bf16[384,768]{1,0:T(8,128)(2,1)}, bf16[384,768]{1,0:T(8,128)(2,1)S(1)}, u32[]{:S(2)}) copy-start(bf16[384,768]{1,0:T(8,128)(2,1)S(1)} %collective-permute-done.2.rest_2_) | copy-start | bytes 1769476
  37.5 5.2 %copy-start.11 = (bf16[512,768]{1,0:T(8,128)(2,1)}, bf16[512,768]{1,0:T(8,128)(2,1)S(1)}, u32[]{:S(2)}) copy-start(bf16[512,768]{1,0:T(8,128)(2,1)S(1)} %collective-permute-done.4.x_ref) | copy-start | bytes 2359300
  37.5 2.0 collective-permute-start.5
  39.5 19.6 %collective-permute-start.6 = (bf16[512,768]{1,0:T(8,128)(2,1)S(1)}, bf16[512,768]{1,0:T(8,128)(2,1)S(1)}, u32[]{:S(2)}, u32[]{:S(2)}) collective-permute-start(bf16[512,768]{1,0:T(8,128)(2,1)S(1)} %get-tuple-element.268), channel_id=1, source_target_pairs={{0,16},{16,0},{1,17},{17,1},{2,18},{18,2},{3,19},{19,3},{4,20},{20... | collective-permute-start | bytes 2359304 | tf_op jit(solution)/shard_map/ppermute | solution.py:772
  96.7 17.1 %copy-start.5 = (bf16[1536,768]{1,0:T(8,128)(2,1)S(1)}, bf16[1536,768]{1,0:T(8,128)(2,1)}, u32[]{:S(2)}) copy-start(bf16[1536,768]{1,0:T(8,128)(2,1)} %get-tuple-element.314) | copy-start | bytes 7077892
  96.7 17.1 %collective-permute-start.7 = (bf16[1536,768]{1,0:T(8,128)(2,1)}, bf16[1536,768]{1,0:T(8,128)(2,1)}, u32[]{:S(2)}, u32[]{:S(2)}) collective-permute-start(bf16[1536,768]{1,0:T(8,128)(2,1)} %get-tuple-element.309), channel_id=1, source_target_pairs={{0,1},{1,0},{2,3},{3,2},{4,5},{5,4},{6,7},{7,6},{8,9},{9,8},{10,11... | collective-permute-start | bytes 7077896 | tf_op jit(solution)/shard_map/ppermute | solution.py:772
  115.3 28.2 %collective-permute-start.8 = (bf16[1536,768]{1,0:T(8,128)(2,1)}, bf16[1536,768]{1,0:T(8,128)(2,1)}, u32[]{:S(2)}, u32[]{:S(2)}) collective-permute-start(bf16[1536,768]{1,0:T(8,128)(2,1)} %get-tuple-element.326), channel_id=1, source_target_pairs={{0,1},{1,0},{2,3},{3,2},{4,5},{5,4},{6,7},{7,6},{8,9},{9,8},{10,11... | collective-permute-start | bytes 7077896 | tf_op jit(solution)/shard_map/ppermute | solution.py:772
  115.7 27.8 %collective-permute-start.10 = (bf16[384,768]{1,0:T(8,128)(2,1)S(1)}, bf16[384,768]{1,0:T(8,128)(2,1)}, u32[]{:S(2)}, u32[]{:S(2)}) collective-permute-start(bf16[384,768]{1,0:T(8,128)(2,1)S(1)} %get-tuple-element.328), channel_id=1, source_target_pairs={{0,4},{1,5},{2,6},{3,7},{4,0},{5,1},{6,2},{7,3},{8,12},{9,13},{10,... | collective-permute-start | bytes 1769480 | tf_op jit(solution)/shard_map/ppermute | solution.py:772
  117.2 26.3 %collective-permute-start.9 = (bf16[384,768]{1,0:T(8,128)(2,1)S(1)}, bf16[384,768]{1,0:T(8,128)(2,1)}, u32[]{:S(2)}, u32[]{:S(2)}) collective-permute-start(bf16[384,768]{1,0:T(8,128)(2,1)S(1)} %get-tuple-element.327), channel_id=1, source_target_pairs={{0,2},{1,3},{2,0},{3,1},{4,6},{5,7},{6,4},{7,5},{8,10},{9,11},{10,... | collective-permute-start | bytes 1769480 | tf_op jit(solution)/shard_map/ppermute | solution.py:772
  148.3 20.7 %collective-permute-start.11 = (bf16[384,768]{1,0:T(8,128)(2,1)}, bf16[384,768]{1,0:T(8,128)(2,1)}, u32[]{:S(2)}, u32[]{:S(2)}) collective-permute-start(bf16[384,768]{1,0:T(8,128)(2,1)} %get-tuple-element.348), channel_id=1, source_target_pairs={{0,1},{1,0},{2,3},{3,2},{4,5},{5,4},{6,7},{7,6},{8,9},{9,8},{10,11... | collective-permute-start | bytes 1769480 | tf_op jit(solution)/shard_map/ppermute | solution.py:772
  148.3 20.7 %collective-permute-start.12 = (bf16[192,768]{1,0:T(8,128)(2,1)}, bf16[192,768]{1,0:T(8,128)(2,1)}, u32[]{:S(2)}, u32[]{:S(2)}) collective-permute-start(bf16[192,768]{1,0:T(8,128)(2,1)} %add_convert_fusion.12), channel_id=1, source_target_pairs={{0,8},{1,9},{2,10},{3,11},{4,12},{5,13},{6,14},{7,15},{8,0},{9,1},... | collective-permute-start | bytes 884744 | tf_op jit(solution)/shard_map/ppermute | solution.py:772
  150.9 31.8 %collective-permute-start.14 = (bf16[768,768]{1,0:T(8,128)(2,1)}, bf16[768,768]{1,0:T(8,128)(2,1)}, u32[]{:S(2)}, u32[]{:S(2)}) collective-permute-start(bf16[768,768]{1,0:T(8,128)(2,1)} %add_convert_fusion.1), channel_id=1, source_target_pairs={{0,2},{1,3},{2,0},{3,1},{4,6},{5,7},{6,4},{7,5},{8,10},{9,11},{10,... | collective-permute-start | bytes 3538952 | tf_op jit(solution)/shard_map/ppermute | solution.py:772
  172.7 9.9 %collective-permute-start.13 = (bf16[192,768]{1,0:T(8,128)(2,1)S(1)}, bf16[192,768]{1,0:T(8,128)(2,1)S(1)}, u32[]{:S(2)}, u32[]{:S(2)}) collective-permute-start(bf16[192,768]{1,0:T(8,128)(2,1)S(1)} %broadcast_select_fusion.2), channel_id=1, source_target_pairs={{0,4},{1,5},{2,6},{3,7},{4,0},{5,1},{6,2},{7,3},{8,12},{9,13},{10,... | collective-permute-start | bytes 884744 | tf_op jit(solution)/shard_map/ppermute | solution.py:772
  173.1 9.5 %copy-start.6 = (bf16[1536,768]{1,0:T(8,128)(2,1)S(1)}, bf16[1536,768]{1,0:T(8,128)(2,1)}, u32[]{:S(2)}) copy-start(bf16[1536,768]{1,0:T(8,128)(2,1)} %get-tuple-element.341) | copy-start | bytes 7077892
  173.1 24.0 %collective-permute-start.17 = (bf16[288,768]{1,0:T(8,128)(2,1)}, bf16[288,768]{1,0:T(8,128)(2,1)}, u32[]{:S(2)}, u32[]{:S(2)}) collective-permute-start(bf16[288,768]{1,0:T(8,128)(2,1)} %pad_maximum_fusion.2), channel_id=1, source_target_pairs={{0,2},{1,3},{2,0},{3,1},{4,6},{5,7},{6,4},{7,5},{8,10},{9,11},{10,... | collective-permute-start | bytes 1327112 | tf_op jit(solution)/shard_map/ppermute | solution.py:772
  186.6 10.6 %collective-permute-start.15 = (bf16[768,768]{1,0:T(8,128)(2,1)}, bf16[768,768]{1,0:T(8,128)(2,1)}, u32[]{:S(2)}, u32[]{:S(2)}) collective-permute-start(bf16[768,768]{1,0:T(8,128)(2,1)} %get-tuple-element.374), channel_id=1, source_target_pairs={{0,1},{1,0},{2,3},{3,2},{4,5},{5,4},{6,7},{7,6},{8,9},{9,8},{10,11... | collective-permute-start | bytes 3538952 | tf_op jit(solution)/shard_map/ppermute | solution.py:772
  186.6 10.6 %collective-permute-start.16 = (bf16[192,768]{1,0:T(8,128)(2,1)}, bf16[192,768]{1,0:T(8,128)(2,1)}, u32[]{:S(2)}, u32[]{:S(2)}) collective-permute-start(bf16[192,768]{1,0:T(8,128)(2,1)} %broadcast_select_fusion.1), channel_id=1, source_target_pairs={{0,4},{1,5},{2,6},{3,7},{4,0},{5,1},{6,2},{7,3},{8,12},{9,13},{10,... | collective-permute-start | bytes 884744 | tf_op jit(solution)/shard_map/ppermute | solution.py:772
  188.2 8.9 %copy-start.2 = (bf16[768,768]{1,0:T(8,128)(2,1)S(1)}, bf16[768,768]{1,0:T(8,128)(2,1)}, u32[]{:S(2)}) copy-start(bf16[768,768]{1,0:T(8,128)(2,1)} %copy-done.1) | copy-start | bytes 3538948
  188.2 9.0 %copy-start.20 = (bf16[384,768]{1,0:T(8,128)(2,1)S(1)}, bf16[384,768]{1,0:T(8,128)(2,1)}, u32[]{:S(2)}) copy-start(bf16[384,768]{1,0:T(8,128)(2,1)} %get-tuple-element.355) | copy-start | bytes 1769476
  201.8 15.9 %copy-start.8 = (f32[192,768]{1,0:T(8,128)S(1)}, f32[192,768]{1,0:T(8,128)}, u32[]{:S(2)}) copy-start(f32[192,768]{1,0:T(8,128)} %copy-done.7) | copy-start | bytes 1769476
  201.8 15.6 %collective-permute-start.18 = (bf16[384,768]{1,0:T(8,128)(2,1)S(1)}, bf16[384,768]{1,0:T(8,128)(2,1)}, u32[]{:S(2)}, u32[]{:S(2)}) collective-permute-start(bf16[384,768]{1,0:T(8,128)(2,1)S(1)} %add_convert_fusion.2), channel_id=1, source_target_pairs={{0,2},{1,3},{2,0},{3,1},{4,6},{5,7},{6,4},{7,5},{8,10},{9,11},{10,... | collective-permute-start | bytes 1769480 | tf_op jit(solution)/shard_map/ppermute | solution.py:772
  202.5 13.6 %collective-permute-start.19 = (bf16[288,768]{1,0:T(8,128)(2,1)S(1)}, bf16[288,768]{1,0:T(8,128)(2,1)}, u32[]{:S(2)}, u32[]{:S(2)}) collective-permute-start(bf16[288,768]{1,0:T(8,128)(2,1)S(1)} %bitcast.98), channel_id=1, source_target_pairs={{0,4},{1,5},{2,6},{3,7},{4,0},{5,1},{6,2},{7,3},{8,12},{9,13},{10,... | collective-permute-start | bytes 1327112 | tf_op jit(solution)/shard_map/ppermute | solution.py:772
  216.1 4.7 %copy-start.12 = (bf16[512,768]{1,0:T(8,128)(2,1)S(1)}, bf16[512,768]{1,0:T(8,128)(2,1)}, u32[]{:S(2)}) copy-start(bf16[512,768]{1,0:T(8,128)(2,1)} %get-tuple-element.400) | copy-start | bytes 2359300
  217.3 3.5 %collective-permute-start.20 = (bf16[512,768]{1,0:T(8,128)(2,1)}, bf16[512,768]{1,0:T(8,128)(2,1)}, u32[]{:S(2)}, u32[]{:S(2)}) collective-permute-start(bf16[512,768]{1,0:T(8,128)(2,1)} %get-tuple-element.403), channel_id=1, source_target_pairs={{0,1},{1,0},{2,3},{3,2},{4,5},{5,4},{6,7},{7,6},{8,9},{9,8},{10,11... | collective-permute-start | bytes 2359304 | tf_op jit(solution)/shard_map/ppermute | solution.py:772
  217.3 31.0 %collective-permute-start.26 = (bf16[192,768]{1,0:T(8,128)(2,1)}, bf16[192,768]{1,0:T(8,128)(2,1)}, u32[]{:S(2)}, u32[]{:S(2)}) collective-permute-start(bf16[192,768]{1,0:T(8,128)(2,1)} %get-tuple-element.416), channel_id=1, source_target_pairs={{0,8},{1,9},{2,10},{3,11},{4,12},{5,13},{6,14},{7,15},{8,0},{9,1},... | collective-permute-start | bytes 884744 | tf_op jit(solution)/shard_map/ppermute | solution.py:772
  219.3 42.8 %collective-permute-start.31 = (bf16[1024,768]{1,0:T(8,128)(2,1)}, bf16[1024,768]{1,0:T(8,128)(2,1)}, u32[]{:S(2)}, u32[]{:S(2)}) collective-permute-start(bf16[1024,768]{1,0:T(8,128)(2,1)} %get-tuple-element.423), channel_id=1, source_target_pairs={{0,16},{16,0},{1,17},{17,1},{2,18},{18,2},{3,19},{19,3},{4,20},{20... | collective-permute-start | bytes 4718600 | tf_op jit(solution)/shard_map/ppermute | solution.py:772
  226.8 18.3 %copy-start.13 = (bf16[512,768]{1,0:T(8,128)(2,1)S(1)}, bf16[512,768]{1,0:T(8,128)(2,1)}, u32[]{:S(2)}) copy-start(bf16[512,768]{1,0:T(8,128)(2,1)} %get-tuple-element.400) | copy-start | bytes 2359300
  226.8 18.3 %collective-permute-start.21 = (bf16[256,768]{1,0:T(8,128)(2,1)}, bf16[256,768]{1,0:T(8,128)(2,1)}, u32[]{:S(2)}, u32[]{:S(2)}) collective-permute-start(bf16[256,768]{1,0:T(8,128)(2,1)} %add_convert_fusion.6), channel_id=1, source_target_pairs={{0,2},{1,3},{2,0},{3,1},{4,6},{5,7},{6,4},{7,5},{8,10},{9,11},{10,... | collective-permute-start | bytes 1179656 | tf_op jit(solution)/shard_map/ppermute | solution.py:772
  230.1 15.1 %collective-permute-start.22 = (bf16[192,768]{1,0:T(8,128)(2,1)}, bf16[192,768]{1,0:T(8,128)(2,1)S(1)}, u32[]{:S(2)}, u32[]{:S(2)}) collective-permute-start(bf16[192,768]{1,0:T(8,128)(2,1)} %add_convert_fusion.7), channel_id=1, source_target_pairs={{0,4},{1,5},{2,6},{3,7},{4,0},{5,1},{6,2},{7,3},{8,12},{9,13},{10,... | collective-permute-start | bytes 884744 | tf_op jit(solution)/shard_map/ppermute | solution.py:772
  231.2 1.2 collective-permute-start.23
  232.3 25.1 %collective-permute-start.29 = (bf16[144,768]{1,0:T(8,128)(2,1)S(1)}, bf16[144,768]{1,0:T(8,128)(2,1)S(1)}, u32[]{:S(2)}, u32[]{:S(2)}) collective-permute-start(bf16[144,768]{1,0:T(8,128)(2,1)S(1)} %fusion.8), channel_id=1, source_target_pairs={{0,8},{1,9},{2,10},{3,11},{4,12},{5,13},{6,14},{7,15},{8,0},{9,1},... | collective-permute-start | bytes 663560 | tf_op jit(solution)/shard_map/ppermute | solution.py:772
  246.2 8.2 %collective-permute-start.24 = (bf16[128,768]{1,0:T(8,128)(2,1)S(1)}, bf16[128,768]{1,0:T(8,128)(2,1)S(1)}, u32[]{:S(2)}, u32[]{:S(2)}) collective-permute-start(bf16[128,768]{1,0:T(8,128)(2,1)S(1)} %add_convert_fusion.13), channel_id=1, source_target_pairs={{0,4},{1,5},{2,6},{3,7},{4,0},{5,1},{6,2},{7,3},{8,12},{9,13},{10,... | collective-permute-start | bytes 589832 | tf_op jit(solution)/shard_map/ppermute | solution.py:772
  246.3 3.7 %collective-permute-start.25 = (f32[1,768]{1,0:T(1,128)S(1)}, f32[1,768]{1,0:T(1,128)S(1)}, u32[]{:S(2)}, u32[]{:S(2)}) collective-permute-start(f32[1,768]{1,0:T(1,128)S(1)} %add.260), channel_id=1, source_target_pairs={{0,2},{1,3},{2,0},{3,1},{4,6},{5,7},{6,4},{7,5},{8,10},{9,11},{10,... | collective-permute-start | bytes 9224 | tf_op jit(solution)/shard_map/ppermute | solution.py:772
  248.3 12.1 %collective-permute-start.30 = (bf16[96,768]{1,0:T(8,128)(2,1)S(1)}, bf16[96,768]{1,0:T(8,128)(2,1)S(1)}, u32[]{:S(2)}, u32[]{:S(2)}) collective-permute-start(bf16[96,768]{1,0:T(8,128)(2,1)S(1)} %add_convert_fusion.14), channel_id=1, source_target_pairs={{0,8},{1,9},{2,10},{3,11},{4,12},{5,13},{6,14},{7,15},{8,0},{9,1},... | collective-permute-start | bytes 442376 | tf_op jit(solution)/shard_map/ppermute | solution.py:772
  255.4 6.7 %collective-permute-start.27 = (bf16[64,768]{1,0:T(8,128)(2,1)S(1)}, bf16[64,768]{1,0:T(8,128)(2,1)S(1)}, u32[]{:S(2)}, u32[]{:S(2)}) collective-permute-start(bf16[64,768]{1,0:T(8,128)(2,1)S(1)} %add_convert_fusion.15), channel_id=1, source_target_pairs={{0,8},{1,9},{2,10},{3,11},{4,12},{5,13},{6,14},{7,15},{8,0},{9,1},... | collective-permute-start | bytes 294920 | tf_op jit(solution)/shard_map/ppermute | solution.py:772
  255.5 5.0 %collective-permute-start.28 = (f32[1,768]{1,0:T(1,128)S(1)}, f32[1,768]{1,0:T(1,128)S(1)}, u32[]{:S(2)}, u32[]{:S(2)}) collective-permute-start(f32[1,768]{1,0:T(1,128)S(1)} %add.265), channel_id=1, source_target_pairs={{0,4},{1,5},{2,6},{3,7},{4,0},{5,1},{6,2},{7,3},{8,12},{9,13},{10,... | collective-permute-start | bytes 9224 | tf_op jit(solution)/shard_map/ppermute | solution.py:772
  264.1 4.7 %copy-start.14 = (f32[48,768]{1,0:T(8,128)S(1)}, f32[48,768]{1,0:T(8,128)}, u32[]{:S(2)}) copy-start(f32[48,768]{1,0:T(8,128)} %get-tuple-element.468) | copy-start | bytes 442372
  266.0 12.7 %collective-permute-start.33 = (f32[64,768]{1,0:T(8,128)S(1)}, f32[64,768]{1,0:T(8,128)S(1)}, u32[]{:S(2)}, u32[]{:S(2)}) collective-permute-start(f32[64,768]{1,0:T(8,128)S(1)} %convert_add_fusion.5), channel_id=1, source_target_pairs={{0,16},{16,0},{1,17},{17,1},{2,18},{18,2},{3,19},{19,3},{4,20},{20... | collective-permute-start | bytes 589832 | tf_op jit(solution)/shard_map/ppermute | solution.py:772
  267.8 10.9 %collective-permute-start.32 = (bf16[96,768]{1,0:T(8,128)(2,1)S(1)}, bf16[96,768]{1,0:T(8,128)(2,1)S(1)}, u32[]{:S(2)}, u32[]{:S(2)}) collective-permute-start(bf16[96,768]{1,0:T(8,128)(2,1)S(1)} %get-tuple-element.435), channel_id=1, source_target_pairs={{0,16},{16,0},{1,17},{17,1},{2,18},{18,2},{3,19},{19,3},{4,20},{20... | collective-permute-start | bytes 442376 | tf_op jit(solution)/shard_map/ppermute | solution.py:772
  268.1 10.6 %collective-permute-start.34 = (f32[1,768]{1,0:T(1,128)S(1)}, f32[1,768]{1,0:T(1,128)S(1)}, u32[]{:S(2)}, u32[]{:S(2)}) collective-permute-start(f32[1,768]{1,0:T(1,128)S(1)} %add.278), channel_id=1, source_target_pairs={{0,8},{1,9},{2,10},{3,11},{4,12},{5,13},{6,14},{7,15},{8,0},{9,1},... | collective-permute-start | bytes 9224 | tf_op jit(solution)/shard_map/ppermute | solution.py:772
  (21 other events, 51.1 us)
